TPU v7x, 256 devices: a whole 4x4x8 slice. The times are simulated.
256 devices in a mesh: dp: 16 (over z, y_hi), ctx: 16 (over x, y_lo, core).
Axes of the slice: x: 4, y: 4 (y_hi: 2, y_lo: 2; y = y_hi * 2 + y_lo), z: 8, core: 2. Of those that a mesh axis runs over, the one named last changes fastest.
Arguments:
- queries: bfloat16 [32768, 2048], P(('dp', 'ctx')), parts along dimension 0, may hold values from -16 to 16
- keys: bfloat16 [32768, 512], P(('dp', 'ctx')), parts along dimension 0, may hold values from -16 to 16
- values: bfloat16 [32768, 512], P(('dp', 'ctx')), parts along dimension 0, may hold values from -6 to 6
- out_grad: bfloat16 [32768, 2048], P(('dp', 'ctx')), parts along dimension 0, may hold values from -6 to 6
- span_of: int32 [512], P('dp'), parts along dimension 0, may hold values from 0 to 31, each once
Outputs:
- query_grad: bfloat16 [32768, 2048], P(('dp', 'ctx')), parts along dimension 0
- key_grad: bfloat16 [32768, 512], P(('dp', 'ctx')), parts along dimension 0
- value_grad: bfloat16 [32768, 512], P(('dp', 'ctx')), parts along dimension 0
There are 16 independent parts, one for each index of `dp`. A program takes and returns all parts, laid end to end along the dimension named above; each array names one. Nothing has to cross between parts.
Inputs may be any that keep to these rules, and one draw needn't show every extreme that they name: `span_of`: each of the 32 spans of the document stands in exactly one half of one device's rows.
All inputs are finite; a program needn't handle non-finite values.
Results may differ from a plain program's by a relative error of at most 0.0069.
Values may be sent and summed in bfloat16 or wider, within the bound.
No kernel may reach another device: no remote copies, remote signals or barrier semaphores. Data moves between devices by JAX's collectives and lax.ppermute only.
A program may use at most 64 MiB of HBM per device.

v0:
```python
import math
from functools import partial

import jax
import jax.numpy as jnp
from jax import lax
from jax.experimental import pallas as pl
from jax.experimental.pallas import tpu as pltpu
from jax.sharding import Mesh, PartitionSpec as P

HEAD = 128
GROUPS = 4
REPEAT = 4
TOK = 128
HALF = 64
SEQ = 2048
TILE = 256
PACK = 2
ROWS = PACK * REPEAT * HALF
WIDE = REPEAT * HEAD
NEG_FILL = -1e30
F32 = jnp.float32
BF16 = jnp.bfloat16
VMEM = pl.BlockSpec(memory_space=pltpu.VMEM)
ANY = pl.BlockSpec(memory_space=pl.ANY)
SMEM = pl.BlockSpec(memory_space=pltpu.SMEM)
PARAMS = pltpu.CompilerParams(vmem_limit_bytes=48 * 1024 * 1024)


LONG = pl.CostEstimate(flops=30_000_000_000, transcendentals=0, bytes_accessed=60_000_000)


def struct(shape, dtype):
    return jax.ShapeDtypeStruct(shape, dtype)


def cut_kv_kernel(keys, values, *pieces):
    x = lax.axis_index("x")
    for step in range(GROUPS):
        column = pl.multiple_of(((x + step) % GROUPS) * HEAD, HEAD)
        pieces[step][:, :HEAD] = keys[:, pl.ds(column, HEAD)]
        pieces[step][:, HEAD:] = values[:, pl.ds(column, HEAD)]


def cut_kv(keys, values):
    return pl.pallas_call(
        cut_kv_kernel,
        out_shape=[struct((TOK, 2 * HEAD), BF16)] * GROUPS,
        in_specs=[VMEM, VMEM],
        out_specs=[VMEM] * GROUPS,
        compiler_params=PARAMS,
        name="cut_kv",
    )(keys, values)


def cut_rows_kernel(queries, out_grad, *pieces):
    x = lax.axis_index("x")
    for step in range(1, GROUPS):
        column = pl.multiple_of(((x + step) % GROUPS) * WIDE, WIDE)
        pieces[step - 1][:, :WIDE] = queries[:, pl.ds(column, WIDE)]
        pieces[step - 1][:, WIDE:] = out_grad[:, pl.ds(column, WIDE)]


def cut_rows(queries, out_grad):
    return pl.pallas_call(
        cut_rows_kernel,
        out_shape=[struct((TOK, 2 * WIDE), BF16)] * (GROUPS - 1),
        in_specs=[VMEM, VMEM],
        out_specs=[VMEM] * (GROUPS - 1),
        compiler_params=PARAMS,
        name="cut_rows",
    )(queries, out_grad)


def arrived_kernel(r1, r2, r3, out):
    out[...] = r1[:8, :HEAD] + r2[:8, :HEAD] + r3[:8, :HEAD]


def arrived(pieces):
    return pl.pallas_call(
        arrived_kernel,
        out_shape=struct((8, HEAD), BF16),
        in_specs=[VMEM] * 3,
        out_specs=VMEM,
        cost_estimate=LONG,
        compiler_params=PARAMS,
        name="rows_arrived",
    )(*pieces)


def nt(a, b):
    return lax.dot_general(a, b, (((1,), (1,)), ((), ())), preferred_element_type=F32)


def nn(a, b):
    return lax.dot_general(a, b, (((1,), (0,)), ((), ())), preferred_element_type=F32)


def fold(tile, op):
    return op(tile.reshape(TILE // 8, 8, ROWS), axis=0)


def attention_kernel(
    spans, token, queries, out_grad, r1, r2, r3, kv00, kv10, kv01, kv11,
    dq0, dq1, dq2, dq3, keep, send,
    ks, vs, kt, rows, dqs, es, ps, dk, dv, order, mine, sems,
):
    x, y, c = lax.axis_index("x"), lax.axis_index("y"), lax.axis_index("c")
    here = pl.ds(pl.multiple_of(x * WIDE, WIDE), WIDE)
    fetches = [
        pltpu.make_async_copy(queries.at[:, here], mine.at[:, :WIDE], sems.at[0]),
        pltpu.make_async_copy(out_grad.at[:, here], mine.at[:, WIDE:], sems.at[1]),
    ]
    for fetch in fetches:
        fetch.start()
    scaling = HEAD ** (-0.5)
    to_base2 = scaling * math.log2(math.e)

    def start_of(step, dy, dc, half):
        owner = ((x - step) % GROUPS) * 4 + (y ^ dy) * 2 + (c ^ dc)
        return spans[2 * owner + half]

    kv_sets = (((0, 0), kv00), ((1, 0), kv10), ((0, 1), kv01), ((1, 1), kv11))
    for (dy, dc), ref in kv_sets:
        for step in range(GROUPS):
            for half in range(2):
                base = pl.multiple_of(start_of(step, dy, dc, half) * HALF, HALF)
                block = ref[step, half * HALF : (half + 1) * HALF]
                ks[pl.ds(base, HALF), :] = block[:, :HEAD]
                vs[pl.ds(base, HALF), :] = block[:, HEAD:]
    for tile in range(SEQ // TILE):
        kt[:, tile * TILE : (tile + 1) * TILE] = ks[tile * TILE : (tile + 1) * TILE].T
    for fetch in fetches:
        fetch.wait()
    for step, ref in enumerate((mine, r1, r2, r3)):
        for half in range(2):
            rows[2 * step + half] = ref[half * HALF : (half + 1) * HALF]
    turns = range(2 * GROUPS)
    own = [start_of(turn // 2, 0, 0, turn % 2) for turn in turns]
    for turn in turns:
        rank = sum((own[other] < own[turn]).astype(jnp.int32) for other in turns)
        order[0, rank] = turn
        order[1, rank] = own[turn]
    dk[...] = jnp.zeros_like(dk)
    dv[...] = jnp.zeros_like(dv)
    key_iota = lax.broadcasted_iota(jnp.int32, (TILE, ROWS), 0)
    lane = lax.broadcasted_iota(jnp.int32, (1, ROWS), 1)

    def one_length(count, limit, turns, q, g):
        at = [slice(tile * TILE, (tile + 1) * TILE) for tile in range(count)]
        peaks = []
        peak = jnp.full((1, ROWS), NEG_FILL, F32)
        total = jnp.zeros((8, ROWS), F32)
        late = ROWS - REPEAT * HALF
        for tile in range(count):
            s = nt(ks[at[tile], :], q) * to_base2
            if tile == count - 1:
                s = jnp.where(key_iota <= limit - tile * TILE, s, NEG_FILL)
            else:
                seen = key_iota[:, :late] <= limit[:, :late] - tile * TILE
                s = jnp.concatenate([jnp.where(seen, s[:, :late], NEG_FILL), s[:, late:]], axis=1)
            top = jnp.maximum(peak, jnp.max(fold(s, jnp.max), axis=0, keepdims=True))
            e = jnp.exp2(s - top)
            es[at[tile], :] = e
            total = total * jnp.exp2(peak - top) + fold(e, jnp.sum)
            peak = top
            peaks.append(peak)
            ps[at[tile], :] = nt(vs[at[tile], :], g)
        inverse = 1.0 / jnp.sum(total, axis=0, keepdims=True)
        shares = [jnp.exp2(old - peak) * inverse for old in peaks]
        delta = jnp.zeros((8, ROWS), F32)
        for tile in range(count):
            w = (es[at[tile], :] * shares[tile]).astype(BF16)
            dv[at[tile], :] += nn(w, g)
            delta += fold(w.astype(F32) * ps[at[tile], :], jnp.sum)
        delta = jnp.sum(delta, axis=0, keepdims=True)
        dq_t = jnp.zeros((HEAD, ROWS), F32)
        for tile in range(count):
            factor = shares[tile] * scaling
            slopes = (es[at[tile], :] * factor * (ps[at[tile], :] - delta)).astype(BF16)
            dk[at[tile], :] += nn(slopes, q)
            dq_t += nn(kt[:, at[tile]], slopes)
        dq = dq_t.T.astype(BF16)
        for index, (turn, h) in enumerate([(turn, h) for turn in turns for h in range(REPEAT)]):
            part = dq[index * HALF : (index + 1) * HALF]
            dqs[turn, :, h * HEAD : (h + 1) * HEAD] = part

    def one_pack(pack, unused):
        turns = [order[0, pack * PACK + i] for i in range(PACK)]
        spans_here = [order[1, pack * PACK + i] for i in range(PACK)]
        tiles = spans_here[-1] * HALF // TILE + 1
        blocks = [rows[turn] for turn in turns]
        cuts = [slice(h * HEAD, (h + 1) * HEAD) for h in range(2 * REPEAT)]
        q = jnp.concatenate([blk[:, cut] for blk in blocks for cut in cuts[:REPEAT]], axis=0)
        g = jnp.concatenate([blk[:, cut] for blk in blocks for cut in cuts[REPEAT:]], axis=0)
        limit = jnp.zeros((1, ROWS), jnp.int32)
        for i in range(PACK):
            limit = jnp.where(lane >= i * REPEAT * HALF, spans_here[i] * HALF, limit)
        limit = limit + lane % HALF
        for count in range(1, SEQ // TILE + 1):
            pl.when(tiles == count)(partial(one_length, count, limit, turns, q, g))
        return unused

    lax.fori_loop(0, 2 * GROUPS // PACK, one_pack, 0)
    for step, ref in enumerate((dq0, dq1, dq2, dq3)):
        for half in range(2):
            ref[half * HALF : (half + 1) * HALF] = dqs[2 * step + half]
    for dc, ref in ((0, keep), (1, send)):
        for chip in range(2 * GROUPS):
            for half in range(2):
                base = pl.multiple_of(spans[4 * chip + 2 * (c ^ dc) + half] * HALF, HALF)
                here = slice(half * HALF, (half + 1) * HALF)
                ref[chip, here, :HEAD] = dk[pl.ds(base, HALF), :].astype(ref.dtype)
                ref[chip, here, HEAD:] = dv[pl.ds(base, HALF), :].astype(ref.dtype)


def attention(spans, token, queries, out_grad, row_pieces, kv_sets):
    return pl.pallas_call(
        attention_kernel,
        out_shape=[struct((TOK, WIDE), BF16)] * GROUPS
        + [
            struct((2 * GROUPS, TOK, 2 * HEAD), F32),
            struct((2 * GROUPS, TOK, 2 * HEAD), BF16),
        ],
        in_specs=[SMEM, VMEM, ANY, ANY] + [VMEM] * 7,
        out_specs=[VMEM] * 6,
        scratch_shapes=[
            pltpu.VMEM((SEQ, HEAD), BF16),
            pltpu.VMEM((SEQ, HEAD), BF16),
            pltpu.VMEM((HEAD, SEQ), BF16),
            pltpu.VMEM((2 * GROUPS, HALF, 2 * WIDE), BF16),
            pltpu.VMEM((2 * GROUPS, HALF, WIDE), BF16),
            pltpu.VMEM((SEQ, ROWS), F32),
            pltpu.VMEM((SEQ, ROWS), F32),
            pltpu.VMEM((SEQ, HEAD), F32),
            pltpu.VMEM((SEQ, HEAD), F32),
            pltpu.SMEM((2, 2 * GROUPS), jnp.int32),
            pltpu.VMEM((TOK, 2 * WIDE), BF16),
            pltpu.SemaphoreType.DMA((2,)),
        ],
        compiler_params=PARAMS,
        name="attention_backward",
    )(spans, token, queries, out_grad, *row_pieces, *kv_sets)


def join_rows_kernel(p0, p1, p2, p3, out):
    x = lax.axis_index("x")
    for step, ref in enumerate((p0, p1, p2, p3)):
        column = pl.multiple_of(((x + step) % GROUPS) * WIDE, WIDE)
        out[:, pl.ds(column, WIDE)] = ref[...]


def join_rows(pieces):
    return pl.pallas_call(
        join_rows_kernel,
        out_shape=struct((TOK, GROUPS * WIDE), BF16),
        in_specs=[VMEM] * GROUPS,
        out_specs=VMEM,
        cost_estimate=LONG,
        compiler_params=PARAMS,
        name="join_rows",
    )(*pieces)


def join_kv(parts):
    split = parts.reshape(GROUPS, 2, TOK, 2 * HEAD).astype(F32)
    total = (split[:, 0] + split[:, 1]).astype(BF16)
    key_grad = total[:, :, :HEAD].transpose(1, 0, 2).reshape(TOK, GROUPS * HEAD)
    value_grad = total[:, :, HEAD:].transpose(1, 0, 2).reshape(TOK, GROUPS * HEAD)
    return key_grad, value_grad


def ahead(block, step):
    return lax.ppermute(block, "x", [(i, (i + step) % GROUPS) for i in range(GROUPS)])


def swap(block, axis):
    return lax.ppermute(block, axis, [(0, 1), (1, 0)])


def on_device(queries, keys, values, out_grad, spans):
    kv0, kv1, kv2, kv3 = cut_kv(keys, values)
    kv_mine = jnp.stack([kv0, ahead(kv1, 1), ahead(kv2, 2), ahead(kv3, 3)])
    rows1, rows2, rows3 = cut_rows(queries, out_grad)
    row_pieces = [ahead(rows1, 1), ahead(rows2, 2), ahead(rows3, 3)]
    token = arrived(row_pieces)
    kv_y = swap(kv_mine, "y")
    kv_c = swap(kv_mine, "c")
    kv_yc = swap(kv_y, "c")
    dq0, dq1, dq2, dq3, keep, send = attention(
        spans, token, queries, out_grad, row_pieces, [kv_mine, kv_y, kv_c, kv_yc]
    )
    total = (keep + swap(send, "c").astype(F32)).astype(BF16)
    home = lax.all_to_all(total, ("x", "y"), 0, 0, tiled=True)
    query_grad = join_rows([dq0, ahead(dq1, 3), ahead(dq2, 2), ahead(dq3, 1)])
    key_grad, value_grad = join_kv(home)
    return query_grad, key_grad, value_grad


def solution(mesh):
    split = Mesh(mesh.devices.reshape(-1, 4, 2, 2), ("dp", "x", "y", "c"))
    whole = P(("dp", "x", "y", "c"), None)
    return jax.shard_map(
        on_device,
        mesh=split,
        in_specs=(whole, whole, whole, whole, P("dp")),
        out_specs=(whole, whole, whole),
        check_vma=False,
    )
```

profile of v0, /device:TPU:160, one launch (start us, length us, event | category | flops | bytes accessed | tf_op | source)
XLA Modules:
  0.0 57.7 jit_solution(5325013041810267776)
XLA Ops:
  0.6 0.0 copy-start.4
  0.6 0.9 %copy-done.4 = bf16[128,512]{1,0:T(8,128)(2,1)S(1)} copy-done((bf16[128,512]{1,0:T(8,128)(2,1)S(1)}, bf16[128,512]{1,0:T(8,128)(2,1)}, u32[]{:S(2)}) %copy-start.4) | copy-done | bytes 131096
  1.5 0.0 copy-start.5
  1.5 0.9 %copy-done.5 = bf16[128,512]{1,0:T(8,128)(2,1)S(1)} copy-done((bf16[128,512]{1,0:T(8,128)(2,1)S(1)}, bf16[128,512]{1,0:T(8,128)(2,1)}, u32[]{:S(2)}) %copy-start.5) | copy-done | bytes 131096
  2.5 1.6 %collective-permute-start.3 = (bf16[128,256]{1,0:T(8,128)(2,1)S(1)}, bf16[128,256]{1,0:T(8,128)(2,1)S(1)}, u32[]{:S(2)}, u32[]{:S(2)}) collective-permute-start(bf16[128,256]{1,0:T(8,128)(2,1)S(1)} %get-tuple-element.20), channel_id=1, source_target_pairs={{0,4},{4,8},{8,12},{12,0},{1,5},{5,9},{9,13},{13,1},{2,6},{6,10},{... | collective-permute-start | bytes 196616 | tf_op jit(solution)/shard_map/ppermute | solution.py:274
  4.1 2.7 %collective-permute-start.4 = (bf16[128,256]{1,0:T(8,128)(2,1)S(1)}, bf16[128,256]{1,0:T(8,128)(2,1)S(1)}, u32[]{:S(2)}, u32[]{:S(2)}) collective-permute-start(bf16[128,256]{1,0:T(8,128)(2,1)S(1)} %get-tuple-element.21), channel_id=1, source_target_pairs={{0,8},{4,12},{8,0},{12,4},{1,9},{5,13},{9,1},{13,5},{2,10},{6,14},... | collective-permute-start | bytes 196616 | tf_op jit(solution)/shard_map/ppermute | solution.py:274
  6.8 1.4 %collective-permute-start.5 = (bf16[128,256]{1,0:T(8,128)(2,1)S(1)}, bf16[128,256]{1,0:T(8,128)(2,1)S(1)}, u32[]{:S(2)}, u32[]{:S(2)}) collective-permute-start(bf16[128,256]{1,0:T(8,128)(2,1)S(1)} %get-tuple-element.22), channel_id=1, source_target_pairs={{0,12},{4,0},{8,4},{12,8},{1,13},{5,1},{9,5},{13,9},{2,14},{6,2},{... | collective-permute-start | bytes 196616 | tf_op jit(solution)/shard_map/ppermute | solution.py:274
  8.2 0.0 copy-start
  8.2 1.0 %copy-done = bf16[128,2048]{1,0:T(8,128)(2,1)S(1)} copy-done((bf16[128,2048]{1,0:T(8,128)(2,1)S(1)}, bf16[128,2048]{1,0:T(8,128)(2,1)}, u32[]{:S(2)}) %copy-start) | copy-done | bytes 524312
  9.3 0.0 copy-start.2
  9.3 1.0 %copy-done.2 = bf16[128,2048]{1,0:T(8,128)(2,1)S(1)} copy-done((bf16[128,2048]{1,0:T(8,128)(2,1)S(1)}, bf16[128,2048]{1,0:T(8,128)(2,1)}, u32[]{:S(2)}) %copy-start.2) | copy-done | bytes 524312
  10.3 0.1 cut_rows.1
  10.4 0.7 %collective-permute-start = (bf16[128,1024]{1,0:T(8,128)(2,1)S(1)}, bf16[128,1024]{1,0:T(8,128)(2,1)S(1)}, u32[]{:S(2)}, u32[]{:S(2)}) collective-permute-start(bf16[128,1024]{1,0:T(8,128)(2,1)S(1)} %get-tuple-element.16), channel_id=1, source_target_pairs={{0,4},{4,8},{8,12},{12,0},{1,5},{5,9},{9,13},{13,1},{2,6},{6,10},{... | collective-permute-start | bytes 786440 | tf_op jit(solution)/shard_map/ppermute | solution.py:274
  11.0 0.0 collective-permute-done.3
  11.0 0.0 collective-permute-done.4
  11.1 0.0 collective-permute-done.5
  11.1 1.7 %collective-permute-start.6 = (bf16[4,128,256]{2,1,0:T(8,128)(2,1)S(1)}, bf16[4,128,256]{2,1,0:T(8,128)(2,1)S(1)}, u32[]{:S(2)}, u32[]{:S(2)}) collective-permute-start(bf16[4,128,256]{2,1,0:T(8,128)(2,1)S(1)} %pad_maximum_fusion.kv00), channel_id=1, source_target_pairs={{0,2},{2,0},{1,3},{3,1},{4,6},{6,4},{5,7},{7,5},{8,10},{10,8},{9,1... | collective-permute-start | bytes 786440 | tf_op jit(solution)/shard_map/ppermute | solution.py:278
  12.8 1.6 %collective-permute-start.1 = (bf16[128,1024]{1,0:T(8,128)(2,1)S(1)}, bf16[128,1024]{1,0:T(8,128)(2,1)S(1)}, u32[]{:S(2)}, u32[]{:S(2)}) collective-permute-start(bf16[128,1024]{1,0:T(8,128)(2,1)S(1)} %get-tuple-element.17), channel_id=1, source_target_pairs={{0,8},{4,12},{8,0},{12,4},{1,9},{5,13},{9,1},{13,5},{2,10},{6,14},... | collective-permute-start | bytes 786440 | tf_op jit(solution)/shard_map/ppermute | solution.py:274
  14.3 0.0 copy-start.1
  14.3 0.0 copy-start.3
  14.3 0.0 copy-start.6
  14.3 1.7 %collective-permute-start.2 = (bf16[128,1024]{1,0:T(8,128)(2,1)S(1)}, bf16[128,1024]{1,0:T(8,128)(2,1)S(1)}, u32[]{:S(2)}, u32[]{:S(2)}) collective-permute-start(bf16[128,1024]{1,0:T(8,128)(2,1)S(1)} %get-tuple-element.18), channel_id=1, source_target_pairs={{0,12},{4,0},{8,4},{12,8},{1,13},{5,1},{9,5},{13,9},{2,14},{6,2},{... | collective-permute-start | bytes 786440 | tf_op jit(solution)/shard_map/ppermute | solution.py:274
  16.0 0.0 collective-permute-start.7
  16.0 2.1 %collective-permute-done.6.kv10 = bf16[4,128,256]{2,1,0:T(8,128)(2,1)S(1)} collective-permute-done((bf16[4,128,256]{2,1,0:T(8,128)(2,1)S(1)}, bf16[4,128,256]{2,1,0:T(8,128)(2,1)S(1)}, u32[]{:S(2)}, u32[]{:S(2)}) %collective-permute-start.6) | collective-permute-done | bytes 262176 | tf_op jit(solution)/shard_map/ppermute | solution.py:278
  18.1 0.0 collective-permute-start.8
  18.1 6.4 %collective-permute-done.r1 = bf16[128,1024]{1,0:T(8,128)(2,1)S(1)} collective-permute-done((bf16[128,1024]{1,0:T(8,128)(2,1)S(1)}, bf16[128,1024]{1,0:T(8,128)(2,1)S(1)}, u32[]{:S(2)}, u32[]{:S(2)}) %collective-permute-start) | collective-permute-done | bytes 262176 | tf_op jit(solution)/shard_map/ppermute | solution.py:274
  24.5 0.0 collective-permute-done.1.r2
  24.5 2.1 %collective-permute-done.2.r3 = bf16[128,1024]{1,0:T(8,128)(2,1)S(1)} collective-permute-done((bf16[128,1024]{1,0:T(8,128)(2,1)S(1)}, bf16[128,1024]{1,0:T(8,128)(2,1)S(1)}, u32[]{:S(2)}, u32[]{:S(2)}) %collective-permute-start.2) | collective-permute-done | bytes 262176 | tf_op jit(solution)/shard_map/ppermute | solution.py:274
  26.6 0.0 collective-permute-done.7.kv01
  26.6 0.0 collective-permute-done.8.kv11
  26.6 0.0 copy-done.1
  26.6 0.0 copy-done.3
  26.6 0.0 copy-done.6
  26.6 12.0 %attention_backward.1 = (bf16[128,512]{1,0:T(8,128)(2,1)S(1)}, bf16[128,512]{1,0:T(8,128)(2,1)S(1)}, bf16[128,512]{1,0:T(8,128)(2,1)S(1)}, bf16[128,512]{1,0:T(8...) custom-call(s32[32]{0:T(128)S(1)} %copy-done.6, bf16[8,128]{1,0:T(8,128)(2,1)S(1)} %rows_arrived.1.token, ...), custom_call_target="tpu_custom_call" | custom-call | tf_op jit(solution)/shard_map/attention_backward/pallas_call | solution.py:218
  38.6 0.1 collective-permute-start.12
  38.7 2.5 %collective-permute-start.9 = (bf16[128,512]{1,0:T(8,128)(2,1)S(1)}, bf16[128,512]{1,0:T(8,128)(2,1)S(1)}, u32[]{:S(2)}, u32[]{:S(2)}) collective-permute-start(bf16[128,512]{1,0:T(8,128)(2,1)S(1)} %get-tuple-element.24), channel_id=1, source_target_pairs={{0,12},{4,0},{8,4},{12,8},{1,13},{5,1},{9,5},{13,9},{2,14},{6,2},{... | collective-permute-start | bytes 393224 | tf_op jit(solution)/shard_map/ppermute | solution.py:274
  41.2 0.0 collective-permute-start.10
  41.2 1.0 %collective-permute-start.11 = (bf16[128,512]{1,0:T(8,128)(2,1)S(1)}, bf16[128,512]{1,0:T(8,128)(2,1)S(1)}, u32[]{:S(2)}, u32[]{:S(2)}) collective-permute-start(bf16[128,512]{1,0:T(8,128)(2,1)S(1)} %get-tuple-element.26), channel_id=1, source_target_pairs={{0,4},{4,8},{8,12},{12,0},{1,5},{5,9},{9,13},{13,1},{2,6},{6,10},{... | collective-permute-start | bytes 393224 | tf_op jit(solution)/shard_map/ppermute | solution.py:274
  42.2 0.0 collective-permute-done.12
  42.2 0.9 %add_convert_fusion = bf16[8,128,256]{2,1,0:T(8,128)(2,1)} fusion(f32[8,128,256]{2,1,0:T(8,128)S(1)} %get-tuple-element.27, bf16[8,128,256]{2,1,0:T(8,128)(2,1)S(1)} %collective-permute-done.12), kind=kLoop, calls=%fused_computation | loop fusion | flops 786432 | bytes 2097152 | tf_op jit(solution)/shard_map/convert_element_type | solution.py:293
  43.1 4.3 %all-to-all-start = ((bf16[8,128,256]{2,1,0:T(8,128)(2,1)}), bf16[8,128,256]{2,1,0:T(8,128)(2,1)S(1)}, u32[]{:S(2)}, u32[]{:S(2)}) async-start(bf16[8,128,256]{2,1,0:T(8,128)(2,1)} %add_convert_fusion), calls=%async_computation | async-start | bytes 1048576 | tf_op jit(solution)/shard_map/all_to_all | solution.py:294
  47.4 0.0 collective-permute-done.9.p1
  47.5 1.7 %collective-permute-done.10.p2 = bf16[128,512]{1,0:T(8,128)(2,1)S(1)} collective-permute-done((bf16[128,512]{1,0:T(8,128)(2,1)S(1)}, bf16[128,512]{1,0:T(8,128)(2,1)S(1)}, u32[]{:S(2)}, u32[]{:S(2)}) %collective-permute-start.10) | collective-permute-done | bytes 131104 | tf_op jit(solution)/shard_map/ppermute | solution.py:274
  49.1 1.7 %collective-permute-done.11.p3 = bf16[128,512]{1,0:T(8,128)(2,1)S(1)} collective-permute-done((bf16[128,512]{1,0:T(8,128)(2,1)S(1)}, bf16[128,512]{1,0:T(8,128)(2,1)S(1)}, u32[]{:S(2)}, u32[]{:S(2)}) %collective-permute-start.11) | collective-permute-done | bytes 131104 | tf_op jit(solution)/shard_map/ppermute | solution.py:274
  50.8 0.9 %join_rows.1 = bf16[128,2048]{1,0:T(8,128)(2,1)} custom-call(bf16[128,512]{1,0:T(8,128)(2,1)S(1)} %get-tuple-element.23.p0, bf16[128,512]{1,0:T(8,128)(2,1)S(1)} %collective-permute-done.9.p1, bf16[128,512]{1,0:T(8,128)(2,1)S(1)} %collective-permute-done.10.p2, bf16[128,512]{1,0:T(8,128)(2,1)S(1)} %collective-permute-done.11.p3), custom_call_target="tpu_custom_call" | custom-call | flops 30000001024 | bytes 60000000 | tf_op jit(solution)/shard_map/join_rows/pallas_call | solution.py:254
  51.6 5.1 %all-to-all-done = bf16[8,128,256]{2,1,0:T(8,128)(2,1)S(1)} async-done(((bf16[8,128,256]{2,1,0:T(8,128)(2,1)}), bf16[8,128,256]{2,1,0:T(8,128)(2,1)S(1)}, u32[]{:S(2)}, u32[]{:S(2)}) %all-to-all-start) | async-done | bytes 524320 | tf_op jit(solution)/shard_map/all_to_all | solution.py:294
  56.8 0.1 convert.1
  56.9 0.1 fusion.1
  57.0 0.7 %copy_bitcast_fusion = (bf16[128,512]{1,0:T(8,128)(2,1)}, bf16[128,512]{1,0:T(8,128)(2,1)}) fusion(bf16[4,16,8,128]{3,2,1,0:T(8,128)(2,1)S(1)} %get-tuple-element.29, bf16[4,16,8,128]{3,2,1,0:T(8,128)(2,1)S(1)} %get-tuple-element.30), kind=kLoop, calls=%fused_computation.5 | loop fusion | bytes 524288 | tf_op jit(solution)/shard_map/reshape | solution.py:269
  (4 shorter events, 0.1 us)
Async XLA Ops:
  0.6 0.9 %copy-start.4 = (bf16[128,512]{1,0:T(8,128)(2,1)S(1)}, bf16[128,512]{1,0:T(8,128)(2,1)}, u32[]{:S(2)}) copy-start(bf16[128,512]{1,0:T(8,128)(2,1)} %keys.1) | copy-start | bytes 393220
  1.5 0.9 %copy-start.5 = (bf16[128,512]{1,0:T(8,128)(2,1)S(1)}, bf16[128,512]{1,0:T(8,128)(2,1)}, u32[]{:S(2)}) copy-start(bf16[128,512]{1,0:T(8,128)(2,1)} %values.1) | copy-start | bytes 393220
  2.5 8.6 %collective-permute-start.3 = (bf16[128,256]{1,0:T(8,128)(2,1)S(1)}, bf16[128,256]{1,0:T(8,128)(2,1)S(1)}, u32[]{:S(2)}, u32[]{:S(2)}) collective-permute-start(bf16[128,256]{1,0:T(8,128)(2,1)S(1)} %get-tuple-element.20), channel_id=1, source_target_pairs={{0,4},{4,8},{8,12},{12,0},{1,5},{5,9},{9,13},{13,1},{2,6},{6,10},{... | collective-permute-start | bytes 196616 | tf_op jit(solution)/shard_map/ppermute | solution.py:274
  4.1 7.0 %collective-permute-start.4 = (bf16[128,256]{1,0:T(8,128)(2,1)S(1)}, bf16[128,256]{1,0:T(8,128)(2,1)S(1)}, u32[]{:S(2)}, u32[]{:S(2)}) collective-permute-start(bf16[128,256]{1,0:T(8,128)(2,1)S(1)} %get-tuple-element.21), channel_id=1, source_target_pairs={{0,8},{4,12},{8,0},{12,4},{1,9},{5,13},{9,1},{13,5},{2,10},{6,14},... | collective-permute-start | bytes 196616 | tf_op jit(solution)/shard_map/ppermute | solution.py:274
  6.8 4.3 %collective-permute-start.5 = (bf16[128,256]{1,0:T(8,128)(2,1)S(1)}, bf16[128,256]{1,0:T(8,128)(2,1)S(1)}, u32[]{:S(2)}, u32[]{:S(2)}) collective-permute-start(bf16[128,256]{1,0:T(8,128)(2,1)S(1)} %get-tuple-element.22), channel_id=1, source_target_pairs={{0,12},{4,0},{8,4},{12,8},{1,13},{5,1},{9,5},{13,9},{2,14},{6,2},{... | collective-permute-start | bytes 196616 | tf_op jit(solution)/shard_map/ppermute | solution.py:274
  8.2 1.0 %copy-start = (bf16[128,2048]{1,0:T(8,128)(2,1)S(1)}, bf16[128,2048]{1,0:T(8,128)(2,1)}, u32[]{:S(2)}) copy-start(bf16[128,2048]{1,0:T(8,128)(2,1)} %queries.3) | copy-start | bytes 1572868
  9.3 1.0 %copy-start.2 = (bf16[128,2048]{1,0:T(8,128)(2,1)S(1)}, bf16[128,2048]{1,0:T(8,128)(2,1)}, u32[]{:S(2)}) copy-start(bf16[128,2048]{1,0:T(8,128)(2,1)} %out_grad.3) | copy-start | bytes 1572868
  10.4 14.1 %collective-permute-start = (bf16[128,1024]{1,0:T(8,128)(2,1)S(1)}, bf16[128,1024]{1,0:T(8,128)(2,1)S(1)}, u32[]{:S(2)}, u32[]{:S(2)}) collective-permute-start(bf16[128,1024]{1,0:T(8,128)(2,1)S(1)} %get-tuple-element.16), channel_id=1, source_target_pairs={{0,4},{4,8},{8,12},{12,0},{1,5},{5,9},{9,13},{13,1},{2,6},{6,10},{... | collective-permute-start | bytes 786440 | tf_op jit(solution)/shard_map/ppermute | solution.py:274
  11.1 7.0 %collective-permute-start.6 = (bf16[4,128,256]{2,1,0:T(8,128)(2,1)S(1)}, bf16[4,128,256]{2,1,0:T(8,128)(2,1)S(1)}, u32[]{:S(2)}, u32[]{:S(2)}) collective-permute-start(bf16[4,128,256]{2,1,0:T(8,128)(2,1)S(1)} %pad_maximum_fusion.kv00), channel_id=1, source_target_pairs={{0,2},{2,0},{1,3},{3,1},{4,6},{6,4},{5,7},{7,5},{8,10},{10,8},{9,1... | collective-permute-start | bytes 786440 | tf_op jit(solution)/shard_map/ppermute | solution.py:278
  12.8 11.7 %collective-permute-start.1 = (bf16[128,1024]{1,0:T(8,128)(2,1)S(1)}, bf16[128,1024]{1,0:T(8,128)(2,1)S(1)}, u32[]{:S(2)}, u32[]{:S(2)}) collective-permute-start(bf16[128,1024]{1,0:T(8,128)(2,1)S(1)} %get-tuple-element.17), channel_id=1, source_target_pairs={{0,8},{4,12},{8,0},{12,4},{1,9},{5,13},{9,1},{13,5},{2,10},{6,14},... | collective-permute-start | bytes 786440 | tf_op jit(solution)/shard_map/ppermute | solution.py:274
  14.3 12.2 %copy-start.1 = (bf16[128,2048]{1,0:T(8,128)(2,1)S(1)}, bf16[128,2048]{1,0:T(8,128)(2,1)}, u32[]{:S(2)}) copy-start(bf16[128,2048]{1,0:T(8,128)(2,1)} %queries.3) | copy-start | bytes 1572868
  14.3 12.2 %copy-start.3 = (bf16[128,2048]{1,0:T(8,128)(2,1)S(1)}, bf16[128,2048]{1,0:T(8,128)(2,1)}, u32[]{:S(2)}) copy-start(bf16[128,2048]{1,0:T(8,128)(2,1)} %out_grad.3) | copy-start | bytes 1572868
  14.3 12.2 %copy-start.6 = (s32[32]{0:T(128)S(1)}, s32[32]{0:T(128)}, u32[]{:S(2)}) copy-start(s32[32]{0:T(128)} %spans.1) | copy-start | bytes 388
  14.3 12.2 %collective-permute-start.2 = (bf16[128,1024]{1,0:T(8,128)(2,1)S(1)}, bf16[128,1024]{1,0:T(8,128)(2,1)S(1)}, u32[]{:S(2)}, u32[]{:S(2)}) collective-permute-start(bf16[128,1024]{1,0:T(8,128)(2,1)S(1)} %get-tuple-element.18), channel_id=1, source_target_pairs={{0,12},{4,0},{8,4},{12,8},{1,13},{5,1},{9,5},{13,9},{2,14},{6,2},{... | collective-permute-start | bytes 786440 | tf_op jit(solution)/shard_map/ppermute | solution.py:274
  16.0 10.5 %collective-permute-start.7 = (bf16[4,128,256]{2,1,0:T(8,128)(2,1)S(1)}, bf16[4,128,256]{2,1,0:T(8,128)(2,1)S(1)}, u32[]{:S(2)}, u32[]{:S(2)}) collective-permute-start(bf16[4,128,256]{2,1,0:T(8,128)(2,1)S(1)} %pad_maximum_fusion.kv00), channel_id=1, source_target_pairs={{0,1},{1,0},{2,3},{3,2},{4,5},{5,4},{6,7},{7,6},{8,9},{9,8},{10,11... | collective-permute-start | bytes 786440 | tf_op jit(solution)/shard_map/ppermute | solution.py:278
  18.1 8.5 %collective-permute-start.8 = (bf16[4,128,256]{2,1,0:T(8,128)(2,1)S(1)}, bf16[4,128,256]{2,1,0:T(8,128)(2,1)S(1)}, u32[]{:S(2)}, u32[]{:S(2)}) collective-permute-start(bf16[4,128,256]{2,1,0:T(8,128)(2,1)S(1)} %collective-permute-done.6.kv10), channel_id=1, source_target_pairs={{0,1},{1,0},{2,3},{3,2},{4,5},{5,4},{6,7},{7,6},{8,9},{9,8},{10,11... | collective-permute-start | bytes 786440 | tf_op jit(solution)/shard_map/ppermute | solution.py:278
  38.6 3.6 %collective-permute-start.12 = (bf16[8,128,256]{2,1,0:T(8,128)(2,1)S(1)}, bf16[8,128,256]{2,1,0:T(8,128)(2,1)S(1)}, u32[]{:S(2)}, u32[]{:S(2)}) collective-permute-start(bf16[8,128,256]{2,1,0:T(8,128)(2,1)S(1)} %get-tuple-element.28), channel_id=1, source_target_pairs={{0,1},{1,0},{2,3},{3,2},{4,5},{5,4},{6,7},{7,6},{8,9},{9,8},{10,11... | collective-permute-start | bytes 1572872 | tf_op jit(solution)/shard_map/ppermute | solution.py:278
  38.7 8.7 %collective-permute-start.9 = (bf16[128,512]{1,0:T(8,128)(2,1)S(1)}, bf16[128,512]{1,0:T(8,128)(2,1)S(1)}, u32[]{:S(2)}, u32[]{:S(2)}) collective-permute-start(bf16[128,512]{1,0:T(8,128)(2,1)S(1)} %get-tuple-element.24), channel_id=1, source_target_pairs={{0,12},{4,0},{8,4},{12,8},{1,13},{5,1},{9,5},{13,9},{2,14},{6,2},{... | collective-permute-start | bytes 393224 | tf_op jit(solution)/shard_map/ppermute | solution.py:274
  41.2 7.9 %collective-permute-start.10 = (bf16[128,512]{1,0:T(8,128)(2,1)S(1)}, bf16[128,512]{1,0:T(8,128)(2,1)S(1)}, u32[]{:S(2)}, u32[]{:S(2)}) collective-permute-start(bf16[128,512]{1,0:T(8,128)(2,1)S(1)} %get-tuple-element.25), channel_id=1, source_target_pairs={{0,8},{4,12},{8,0},{12,4},{1,9},{5,13},{9,1},{13,5},{2,10},{6,14},... | collective-permute-start | bytes 393224 | tf_op jit(solution)/shard_map/ppermute | solution.py:274
  41.2 9.6 %collective-permute-start.11 = (bf16[128,512]{1,0:T(8,128)(2,1)S(1)}, bf16[128,512]{1,0:T(8,128)(2,1)S(1)}, u32[]{:S(2)}, u32[]{:S(2)}) collective-permute-start(bf16[128,512]{1,0:T(8,128)(2,1)S(1)} %get-tuple-element.26), channel_id=1, source_target_pairs={{0,4},{4,8},{8,12},{12,0},{1,5},{5,9},{9,13},{13,1},{2,6},{6,10},{... | collective-permute-start | bytes 393224 | tf_op jit(solution)/shard_map/ppermute | solution.py:274
  43.1 13.7 %all-to-all-start = ((bf16[8,128,256]{2,1,0:T(8,128)(2,1)}), bf16[8,128,256]{2,1,0:T(8,128)(2,1)S(1)}, u32[]{:S(2)}, u32[]{:S(2)}) async-start(bf16[8,128,256]{2,1,0:T(8,128)(2,1)} %add_convert_fusion), calls=%async_computation | async-start | bytes 1048576 | tf_op jit(solution)/shard_map/all_to_all | solution.py:294
where the time goes:
time: 58.5 us; the launch traced here: 57.7 us
  starting transfers between devices  19.2 us (33%)
  waiting for transfers between devices  19 us (32%)
  Pallas kernels  13 us (22%)
  local copies, waits for them, and re-layouts  4.67 us (8%)
  other arithmetic  1.1 us (2%)
  between operations  0.75 us (1%)
    ppermute x9, starting transfers between devices, ahead(): lax.ppermute(block, 'x', [(i, (i + step) % GROUPS) for i in range(GROUPS)])  13.1 us
    pallas_call x1, Pallas kernels, attention(): pl.pallas_call(attention_kernel, out_shape=[struct((TOK, WIDE), BF16)] *...  12 us
    ppermute x9, waiting for transfers between devices, ahead(): lax.ppermute(block, 'x', [(i, (i + step) % GROUPS) for i in range(GROUPS)])  11.8 us
    all_to_all x1, waiting for transfers between devices, on_device(): home = lax.all_to_all(total, ('x', 'y'), 0, 0, tiled=True)  5.12 us
    all_to_all x1, starting transfers between devices, on_device(): home = lax.all_to_all(total, ('x', 'y'), 0, 0, tiled=True)  4.35 us
    unnamed x15, local copies, waits for them, and re-layouts  3.94 us
    ppermute x4, waiting for transfers between devices, swap(): return lax.ppermute(block, axis, [(0, 1), (1, 0)])  2.1 us
    ppermute x4, starting transfers between devices, swap(): return lax.ppermute(block, axis, [(0, 1), (1, 0)])  1.76 us
  transfers between devices with their start and end apart: 14, of which 6 were waited for; matrix products, arithmetic and copies ran while one was open for 2% of the time, Pallas kernels for 2%

commit v1 on v0

--- a/solution.py
+++ b/solution.py
@@ -243,9 +243,9 @@
     )(spans, token, queries, out_grad, *row_pieces, *kv_sets)
 
 
-def join_rows_kernel(p0, p1, p2, p3, out):
+def join_rows_kernel(p0, p2, p1, p3, out):
     x = lax.axis_index("x")
-    for step, ref in enumerate((p0, p1, p2, p3)):
+    for step, ref in ((0, p0), (2, p2), (1, p1), (3, p3)):
         column = pl.multiple_of(((x + step) % GROUPS) * WIDE, WIDE)
         out[:, pl.ds(column, WIDE)] = ref[...]
 
@@ -282,8 +282,10 @@
     kv0, kv1, kv2, kv3 = cut_kv(keys, values)
     kv_mine = jnp.stack([kv0, ahead(kv1, 1), ahead(kv2, 2), ahead(kv3, 3)])
     rows1, rows2, rows3 = cut_rows(queries, out_grad)
-    row_pieces = [ahead(rows1, 1), ahead(rows2, 2), ahead(rows3, 3)]
-    token = arrived(row_pieces)
+    r2 = ahead(rows2, 2)
+    r1, r3 = ahead(rows1, 1), ahead(rows3, 3)
+    row_pieces = [r1, r2, r3]
+    token = arrived([r2, r1, r3])
     kv_y = swap(kv_mine, "y")
     kv_c = swap(kv_mine, "c")
     kv_yc = swap(kv_y, "c")
@@ -292,7 +294,9 @@
     )
     total = (keep + swap(send, "c").astype(F32)).astype(BF16)
     home = lax.all_to_all(total, ("x", "y"), 0, 0, tiled=True)
-    query_grad = join_rows([dq0, ahead(dq1, 3), ahead(dq2, 2), ahead(dq3, 1)])
+    home2 = ahead(dq2, 2)
+    home1, home3 = ahead(dq1, 3), ahead(dq3, 1)
+    query_grad = join_rows([dq0, home2, home1, home3])
     key_grad, value_grad = join_kv(home)
     return query_grad, key_grad, value_grad
 

time: 58.5 us -> 58.3 us (level)
  the two profiles are of different devices: /device:TPU:160 before, /device:TPU:64 now
where the time goes in v1:
time: 58.3 us; the launch traced here: 58.5 us
  starting transfers between devices  24 us (41%)
  waiting for transfers between devices  17.2 us (30%)
  Pallas kernels  10.7 us (18%)
  local copies, waits for them, and re-layouts  4.67 us (8%)
  other arithmetic  1.1 us (2%)
  between operations  0.77 us (1%)
    ppermute x9, starting transfers between devices, ahead(): lax.ppermute(block, 'x', [(i, (i + step) % GROUPS) for i in range(GROUPS)])  12.9 us
    pallas_call x1, Pallas kernels, attention(): pl.pallas_call(attention_kernel, out_shape=[struct((TOK, WIDE), BF16)] *...  9.73 us
    all_to_all x1, starting transfers between devices, on_device(): home = lax.all_to_all(total, ('x', 'y'), 0, 0, tiled=True)  9.33 us
    all_to_all x1, waiting for transfers between devices, on_device(): home = lax.all_to_all(total, ('x', 'y'), 0, 0, tiled=True)  8.34 us
    ppermute x9, waiting for transfers between devices, ahead(): lax.ppermute(block, 'x', [(i, (i + step) % GROUPS) for i in range(GROUPS)])  6.83 us
    unnamed x15, local copies, waits for them, and re-layouts  3.94 us
    ppermute x4, waiting for transfers between devices, swap(): return lax.ppermute(block, axis, [(0, 1), (1, 0)])  2.06 us
    ppermute x4, starting transfers between devices, swap(): return lax.ppermute(block, axis, [(0, 1), (1, 0)])  1.76 us
  transfers between devices with their start and end apart: 14, of which 5 were waited for; matrix products, arithmetic and copies ran while one was open for 2% of the time, Pallas kernels for 2%

profile of v1, /device:TPU:64, one launch (start us, length us, event | category | flops | bytes accessed | tf_op | source)
XLA Modules:
  0.0 58.5 jit_solution(14819031680523063822)
XLA Ops:
  0.6 0.0 copy-start.4
  0.6 0.9 %copy-done.4 = bf16[128,512]{1,0:T(8,128)(2,1)S(1)} copy-done((bf16[128,512]{1,0:T(8,128)(2,1)S(1)}, bf16[128,512]{1,0:T(8,128)(2,1)}, u32[]{:S(2)}) %copy-start.4) | copy-done | bytes 131096
  1.5 0.0 copy-start.5
  1.5 0.9 %copy-done.5 = bf16[128,512]{1,0:T(8,128)(2,1)S(1)} copy-done((bf16[128,512]{1,0:T(8,128)(2,1)S(1)}, bf16[128,512]{1,0:T(8,128)(2,1)}, u32[]{:S(2)}) %copy-start.5) | copy-done | bytes 131096
  2.5 1.6 %collective-permute-start.3 = (bf16[128,256]{1,0:T(8,128)(2,1)S(1)}, bf16[128,256]{1,0:T(8,128)(2,1)S(1)}, u32[]{:S(2)}, u32[]{:S(2)}) collective-permute-start(bf16[128,256]{1,0:T(8,128)(2,1)S(1)} %get-tuple-element.20), channel_id=1, source_target_pairs={{0,4},{4,8},{8,12},{12,0},{1,5},{5,9},{9,13},{13,1},{2,6},{6,10},{... | collective-permute-start | bytes 196616 | tf_op jit(solution)/shard_map/ppermute | solution.py:274
  4.1 2.7 %collective-permute-start.4 = (bf16[128,256]{1,0:T(8,128)(2,1)S(1)}, bf16[128,256]{1,0:T(8,128)(2,1)S(1)}, u32[]{:S(2)}, u32[]{:S(2)}) collective-permute-start(bf16[128,256]{1,0:T(8,128)(2,1)S(1)} %get-tuple-element.21), channel_id=1, source_target_pairs={{0,8},{4,12},{8,0},{12,4},{1,9},{5,13},{9,1},{13,5},{2,10},{6,14},... | collective-permute-start | bytes 196616 | tf_op jit(solution)/shard_map/ppermute | solution.py:274
  6.8 1.4 %collective-permute-start.5 = (bf16[128,256]{1,0:T(8,128)(2,1)S(1)}, bf16[128,256]{1,0:T(8,128)(2,1)S(1)}, u32[]{:S(2)}, u32[]{:S(2)}) collective-permute-start(bf16[128,256]{1,0:T(8,128)(2,1)S(1)} %get-tuple-element.22), channel_id=1, source_target_pairs={{0,12},{4,0},{8,4},{12,8},{1,13},{5,1},{9,5},{13,9},{2,14},{6,2},{... | collective-permute-start | bytes 196616 | tf_op jit(solution)/shard_map/ppermute | solution.py:274
  8.2 0.0 copy-start
  8.2 1.0 %copy-done = bf16[128,2048]{1,0:T(8,128)(2,1)S(1)} copy-done((bf16[128,2048]{1,0:T(8,128)(2,1)S(1)}, bf16[128,2048]{1,0:T(8,128)(2,1)}, u32[]{:S(2)}) %copy-start) | copy-done | bytes 524312
  9.3 0.0 copy-start.2
  9.3 1.0 %copy-done.2 = bf16[128,2048]{1,0:T(8,128)(2,1)S(1)} copy-done((bf16[128,2048]{1,0:T(8,128)(2,1)S(1)}, bf16[128,2048]{1,0:T(8,128)(2,1)}, u32[]{:S(2)}) %copy-start.2) | copy-done | bytes 524312
  10.3 0.1 cut_rows.1
  10.4 0.6 %collective-permute-start = (bf16[128,1024]{1,0:T(8,128)(2,1)S(1)}, bf16[128,1024]{1,0:T(8,128)(2,1)S(1)}, u32[]{:S(2)}, u32[]{:S(2)}) collective-permute-start(bf16[128,1024]{1,0:T(8,128)(2,1)S(1)} %get-tuple-element.16), channel_id=1, source_target_pairs={{0,8},{4,12},{8,0},{12,4},{1,9},{5,13},{9,1},{13,5},{2,10},{6,14},... | collective-permute-start | bytes 786440 | tf_op jit(solution)/shard_map/ppermute | solution.py:274
  11.0 0.0 collective-permute-done.3
  11.0 0.0 collective-permute-done.4
  11.0 0.1 collective-permute-done.5
  11.1 1.7 %collective-permute-start.6 = (bf16[4,128,256]{2,1,0:T(8,128)(2,1)S(1)}, bf16[4,128,256]{2,1,0:T(8,128)(2,1)S(1)}, u32[]{:S(2)}, u32[]{:S(2)}) collective-permute-start(bf16[4,128,256]{2,1,0:T(8,128)(2,1)S(1)} %pad_maximum_fusion.kv00), channel_id=1, source_target_pairs={{0,2},{2,0},{1,3},{3,1},{4,6},{6,4},{5,7},{7,5},{8,10},{10,8},{9,1... | collective-permute-start | bytes 786440 | tf_op jit(solution)/shard_map/ppermute | solution.py:278
  12.8 0.6 collective-permute-start.1
  13.3 0.0 copy-start.1
  13.3 0.0 copy-start.3
  13.3 0.0 copy-start.6
  13.3 2.7 %collective-permute-start.2 = (bf16[128,1024]{1,0:T(8,128)(2,1)S(1)}, bf16[128,1024]{1,0:T(8,128)(2,1)S(1)}, u32[]{:S(2)}, u32[]{:S(2)}) collective-permute-start(bf16[128,1024]{1,0:T(8,128)(2,1)S(1)} %get-tuple-element.18), channel_id=1, source_target_pairs={{0,12},{4,0},{8,4},{12,8},{1,13},{5,1},{9,5},{13,9},{2,14},{6,2},{... | collective-permute-start | bytes 786440 | tf_op jit(solution)/shard_map/ppermute | solution.py:274
  16.0 0.0 collective-permute-start.7
  16.0 2.1 %collective-permute-done.6.kv10 = bf16[4,128,256]{2,1,0:T(8,128)(2,1)S(1)} collective-permute-done((bf16[4,128,256]{2,1,0:T(8,128)(2,1)S(1)}, bf16[4,128,256]{2,1,0:T(8,128)(2,1)S(1)}, u32[]{:S(2)}, u32[]{:S(2)}) %collective-permute-start.6) | collective-permute-done | bytes 262176 | tf_op jit(solution)/shard_map/ppermute | solution.py:278
  18.1 0.0 collective-permute-start.8
  18.1 3.2 %collective-permute-done.r1.r2 = bf16[128,1024]{1,0:T(8,128)(2,1)S(1)} collective-permute-done((bf16[128,1024]{1,0:T(8,128)(2,1)S(1)}, bf16[128,1024]{1,0:T(8,128)(2,1)S(1)}, u32[]{:S(2)}, u32[]{:S(2)}) %collective-permute-start) | collective-permute-done | bytes 262176 | tf_op jit(solution)/shard_map/ppermute | solution.py:274
  21.3 3.5 %collective-permute-done.1.r2.r1 = bf16[128,1024]{1,0:T(8,128)(2,1)S(1)} collective-permute-done((bf16[128,1024]{1,0:T(8,128)(2,1)S(1)}, bf16[128,1024]{1,0:T(8,128)(2,1)S(1)}, u32[]{:S(2)}, u32[]{:S(2)}) %collective-permute-start.1) | collective-permute-done | bytes 262176 | tf_op jit(solution)/shard_map/ppermute | solution.py:274
  24.8 0.0 collective-permute-done.2.r3
  24.8 0.0 collective-permute-done.7.kv01
  24.8 0.0 collective-permute-done.8.kv11
  24.8 0.0 copy-done.1
  24.8 0.0 copy-done.3
  24.8 0.0 copy-done.6
  24.8 9.7 %attention_backward.1 = (bf16[128,512]{1,0:T(8,128)(2,1)S(1)}, bf16[128,512]{1,0:T(8,128)(2,1)S(1)}, bf16[128,512]{1,0:T(8,128)(2,1)S(1)}, bf16[128,512]{1,0:T(8...) custom-call(s32[32]{0:T(128)S(1)} %copy-done.6, bf16[8,128]{1,0:T(8,128)(2,1)S(1)} %rows_arrived.1.token, ...), custom_call_target="tpu_custom_call" | custom-call | tf_op jit(solution)/shard_map/attention_backward/pallas_call | solution.py:218
  34.6 0.1 collective-permute-start.12
  34.7 1.3 %collective-permute-start.9 = (bf16[128,512]{1,0:T(8,128)(2,1)S(1)}, bf16[128,512]{1,0:T(8,128)(2,1)S(1)}, u32[]{:S(2)}, u32[]{:S(2)}) collective-permute-start(bf16[128,512]{1,0:T(8,128)(2,1)S(1)} %get-tuple-element.24), channel_id=1, source_target_pairs={{0,8},{4,12},{8,0},{12,4},{1,9},{5,13},{9,1},{13,5},{2,10},{6,14},... | collective-permute-start | bytes 393224 | tf_op jit(solution)/shard_map/ppermute | solution.py:274
  36.0 2.1 %collective-permute-start.10 = (bf16[128,512]{1,0:T(8,128)(2,1)S(1)}, bf16[128,512]{1,0:T(8,128)(2,1)S(1)}, u32[]{:S(2)}, u32[]{:S(2)}) collective-permute-start(bf16[128,512]{1,0:T(8,128)(2,1)S(1)} %get-tuple-element.25), channel_id=1, source_target_pairs={{0,12},{4,0},{8,4},{12,8},{1,13},{5,1},{9,5},{13,9},{2,14},{6,2},{... | collective-permute-start | bytes 393224 | tf_op jit(solution)/shard_map/ppermute | solution.py:274
  38.0 0.0 collective-permute-start.11
  38.0 0.0 collective-permute-done.12
  38.0 0.9 %add_convert_fusion = bf16[8,128,256]{2,1,0:T(8,128)(2,1)} fusion(f32[8,128,256]{2,1,0:T(8,128)S(1)} %get-tuple-element.27, bf16[8,128,256]{2,1,0:T(8,128)(2,1)S(1)} %collective-permute-done.12), kind=kLoop, calls=%fused_computation | loop fusion | flops 786432 | bytes 2097152 | tf_op jit(solution)/shard_map/convert_element_type | solution.py:295
  39.0 9.3 %all-to-all-start = ((bf16[8,128,256]{2,1,0:T(8,128)(2,1)}), bf16[8,128,256]{2,1,0:T(8,128)(2,1)S(1)}, u32[]{:S(2)}, u32[]{:S(2)}) async-start(bf16[8,128,256]{2,1,0:T(8,128)(2,1)} %add_convert_fusion), calls=%async_computation | async-start | bytes 1048576 | tf_op jit(solution)/shard_map/all_to_all | solution.py:296
  48.3 0.0 collective-permute-done.9.p2
  48.3 0.0 collective-permute-done.10.p1
  48.3 0.0 collective-permute-done.11.p3
  48.3 0.9 %join_rows.1 = bf16[128,2048]{1,0:T(8,128)(2,1)} custom-call(bf16[128,512]{1,0:T(8,128)(2,1)S(1)} %get-tuple-element.23.p0, bf16[128,512]{1,0:T(8,128)(2,1)S(1)} %collective-permute-done.9.p2, bf16[128,512]{1,0:T(8,128)(2,1)S(1)} %collective-permute-done.10.p1, bf16[128,512]{1,0:T(8,128)(2,1)S(1)} %collective-permute-done.11.p3), custom_call_target="tpu_custom_call" | custom-call | flops 30000001024 | bytes 60000000 | tf_op jit(solution)/shard_map/join_rows/pallas_call | solution.py:254
  49.2 8.3 %all-to-all-done = bf16[8,128,256]{2,1,0:T(8,128)(2,1)S(1)} async-done(((bf16[8,128,256]{2,1,0:T(8,128)(2,1)}), bf16[8,128,256]{2,1,0:T(8,128)(2,1)S(1)}, u32[]{:S(2)}, u32[]{:S(2)}) %all-to-all-start) | async-done | bytes 524320 | tf_op jit(solution)/shard_map/all_to_all | solution.py:296
  57.5 0.1 convert.1
  57.6 0.1 fusion.1
  57.7 0.7 %copy_bitcast_fusion = (bf16[128,512]{1,0:T(8,128)(2,1)}, bf16[128,512]{1,0:T(8,128)(2,1)}) fusion(bf16[4,16,8,128]{3,2,1,0:T(8,128)(2,1)S(1)} %get-tuple-element.29, bf16[4,16,8,128]{3,2,1,0:T(8,128)(2,1)S(1)} %get-tuple-element.30), kind=kLoop, calls=%fused_computation.5 | loop fusion | bytes 524288 | tf_op jit(solution)/shard_map/reshape | solution.py:269
  (4 shorter events, 0.1 us)
Async XLA Ops:
  0.6 0.9 %copy-start.4 = (bf16[128,512]{1,0:T(8,128)(2,1)S(1)}, bf16[128,512]{1,0:T(8,128)(2,1)}, u32[]{:S(2)}) copy-start(bf16[128,512]{1,0:T(8,128)(2,1)} %keys.1) | copy-start | bytes 393220
  1.5 0.9 %copy-start.5 = (bf16[128,512]{1,0:T(8,128)(2,1)S(1)}, bf16[128,512]{1,0:T(8,128)(2,1)}, u32[]{:S(2)}) copy-start(bf16[128,512]{1,0:T(8,128)(2,1)} %values.1) | copy-start | bytes 393220
  2.5 8.5 %collective-permute-start.3 = (bf16[128,256]{1,0:T(8,128)(2,1)S(1)}, bf16[128,256]{1,0:T(8,128)(2,1)S(1)}, u32[]{:S(2)}, u32[]{:S(2)}) collective-permute-start(bf16[128,256]{1,0:T(8,128)(2,1)S(1)} %get-tuple-element.20), channel_id=1, source_target_pairs={{0,4},{4,8},{8,12},{12,0},{1,5},{5,9},{9,13},{13,1},{2,6},{6,10},{... | collective-permute-start | bytes 196616 | tf_op jit(solution)/shard_map/ppermute | solution.py:274
  4.1 6.9 %collective-permute-start.4 = (bf16[128,256]{1,0:T(8,128)(2,1)S(1)}, bf16[128,256]{1,0:T(8,128)(2,1)S(1)}, u32[]{:S(2)}, u32[]{:S(2)}) collective-permute-start(bf16[128,256]{1,0:T(8,128)(2,1)S(1)} %get-tuple-element.21), channel_id=1, source_target_pairs={{0,8},{4,12},{8,0},{12,4},{1,9},{5,13},{9,1},{13,5},{2,10},{6,14},... | collective-permute-start | bytes 196616 | tf_op jit(solution)/shard_map/ppermute | solution.py:274
  6.8 4.3 %collective-permute-start.5 = (bf16[128,256]{1,0:T(8,128)(2,1)S(1)}, bf16[128,256]{1,0:T(8,128)(2,1)S(1)}, u32[]{:S(2)}, u32[]{:S(2)}) collective-permute-start(bf16[128,256]{1,0:T(8,128)(2,1)S(1)} %get-tuple-element.22), channel_id=1, source_target_pairs={{0,12},{4,0},{8,4},{12,8},{1,13},{5,1},{9,5},{13,9},{2,14},{6,2},{... | collective-permute-start | bytes 196616 | tf_op jit(solution)/shard_map/ppermute | solution.py:274
  8.2 1.0 %copy-start = (bf16[128,2048]{1,0:T(8,128)(2,1)S(1)}, bf16[128,2048]{1,0:T(8,128)(2,1)}, u32[]{:S(2)}) copy-start(bf16[128,2048]{1,0:T(8,128)(2,1)} %queries.3) | copy-start | bytes 1572868
  9.3 1.0 %copy-start.2 = (bf16[128,2048]{1,0:T(8,128)(2,1)S(1)}, bf16[128,2048]{1,0:T(8,128)(2,1)}, u32[]{:S(2)}) copy-start(bf16[128,2048]{1,0:T(8,128)(2,1)} %out_grad.3) | copy-start | bytes 1572868
  10.4 10.9 %collective-permute-start = (bf16[128,1024]{1,0:T(8,128)(2,1)S(1)}, bf16[128,1024]{1,0:T(8,128)(2,1)S(1)}, u32[]{:S(2)}, u32[]{:S(2)}) collective-permute-start(bf16[128,1024]{1,0:T(8,128)(2,1)S(1)} %get-tuple-element.16), channel_id=1, source_target_pairs={{0,8},{4,12},{8,0},{12,4},{1,9},{5,13},{9,1},{13,5},{2,10},{6,14},... | collective-permute-start | bytes 786440 | tf_op jit(solution)/shard_map/ppermute | solution.py:274
  11.1 7.0 %collective-permute-start.6 = (bf16[4,128,256]{2,1,0:T(8,128)(2,1)S(1)}, bf16[4,128,256]{2,1,0:T(8,128)(2,1)S(1)}, u32[]{:S(2)}, u32[]{:S(2)}) collective-permute-start(bf16[4,128,256]{2,1,0:T(8,128)(2,1)S(1)} %pad_maximum_fusion.kv00), channel_id=1, source_target_pairs={{0,2},{2,0},{1,3},{3,1},{4,6},{6,4},{5,7},{7,5},{8,10},{10,8},{9,1... | collective-permute-start | bytes 786440 | tf_op jit(solution)/shard_map/ppermute | solution.py:278
  12.8 12.0 %collective-permute-start.1 = (bf16[128,1024]{1,0:T(8,128)(2,1)S(1)}, bf16[128,1024]{1,0:T(8,128)(2,1)S(1)}, u32[]{:S(2)}, u32[]{:S(2)}) collective-permute-start(bf16[128,1024]{1,0:T(8,128)(2,1)S(1)} %get-tuple-element.17), channel_id=1, source_target_pairs={{0,4},{4,8},{8,12},{12,0},{1,5},{5,9},{9,13},{13,1},{2,6},{6,10},{... | collective-permute-start | bytes 786440 | tf_op jit(solution)/shard_map/ppermute | solution.py:274
  13.3 11.5 %copy-start.1 = (bf16[128,2048]{1,0:T(8,128)(2,1)S(1)}, bf16[128,2048]{1,0:T(8,128)(2,1)}, u32[]{:S(2)}) copy-start(bf16[128,2048]{1,0:T(8,128)(2,1)} %queries.3) | copy-start | bytes 1572868
  13.3 11.5 %copy-start.3 = (bf16[128,2048]{1,0:T(8,128)(2,1)S(1)}, bf16[128,2048]{1,0:T(8,128)(2,1)}, u32[]{:S(2)}) copy-start(bf16[128,2048]{1,0:T(8,128)(2,1)} %out_grad.3) | copy-start | bytes 1572868
  13.3 11.5 %copy-start.6 = (s32[32]{0:T(128)S(1)}, s32[32]{0:T(128)}, u32[]{:S(2)}) copy-start(s32[32]{0:T(128)} %spans.1) | copy-start | bytes 388
  13.3 11.4 %collective-permute-start.2 = (bf16[128,1024]{1,0:T(8,128)(2,1)S(1)}, bf16[128,1024]{1,0:T(8,128)(2,1)S(1)}, u32[]{:S(2)}, u32[]{:S(2)}) collective-permute-start(bf16[128,1024]{1,0:T(8,128)(2,1)S(1)} %get-tuple-element.18), channel_id=1, source_target_pairs={{0,12},{4,0},{8,4},{12,8},{1,13},{5,1},{9,5},{13,9},{2,14},{6,2},{... | collective-permute-start | bytes 786440 | tf_op jit(solution)/shard_map/ppermute | solution.py:274
  16.0 8.8 %collective-permute-start.7 = (bf16[4,128,256]{2,1,0:T(8,128)(2,1)S(1)}, bf16[4,128,256]{2,1,0:T(8,128)(2,1)S(1)}, u32[]{:S(2)}, u32[]{:S(2)}) collective-permute-start(bf16[4,128,256]{2,1,0:T(8,128)(2,1)S(1)} %pad_maximum_fusion.kv00), channel_id=1, source_target_pairs={{0,1},{1,0},{2,3},{3,2},{4,5},{5,4},{6,7},{7,6},{8,9},{9,8},{10,11... | collective-permute-start | bytes 786440 | tf_op jit(solution)/shard_map/ppermute | solution.py:278
  18.1 6.7 %collective-permute-start.8 = (bf16[4,128,256]{2,1,0:T(8,128)(2,1)S(1)}, bf16[4,128,256]{2,1,0:T(8,128)(2,1)S(1)}, u32[]{:S(2)}, u32[]{:S(2)}) collective-permute-start(bf16[4,128,256]{2,1,0:T(8,128)(2,1)S(1)} %collective-permute-done.6.kv10), channel_id=1, source_target_pairs={{0,1},{1,0},{2,3},{3,2},{4,5},{5,4},{6,7},{7,6},{8,9},{9,8},{10,11... | collective-permute-start | bytes 786440 | tf_op jit(solution)/shard_map/ppermute | solution.py:278
  34.6 3.4 %collective-permute-start.12 = (bf16[8,128,256]{2,1,0:T(8,128)(2,1)S(1)}, bf16[8,128,256]{2,1,0:T(8,128)(2,1)S(1)}, u32[]{:S(2)}, u32[]{:S(2)}) collective-permute-start(bf16[8,128,256]{2,1,0:T(8,128)(2,1)S(1)} %get-tuple-element.28), channel_id=1, source_target_pairs={{0,1},{1,0},{2,3},{3,2},{4,5},{5,4},{6,7},{7,6},{8,9},{9,8},{10,11... | collective-permute-start | bytes 1572872 | tf_op jit(solution)/shard_map/ppermute | solution.py:278
  34.7 13.6 %collective-permute-start.9 = (bf16[128,512]{1,0:T(8,128)(2,1)S(1)}, bf16[128,512]{1,0:T(8,128)(2,1)S(1)}, u32[]{:S(2)}, u32[]{:S(2)}) collective-permute-start(bf16[128,512]{1,0:T(8,128)(2,1)S(1)} %get-tuple-element.24), channel_id=1, source_target_pairs={{0,8},{4,12},{8,0},{12,4},{1,9},{5,13},{9,1},{13,5},{2,10},{6,14},... | collective-permute-start | bytes 393224 | tf_op jit(solution)/shard_map/ppermute | solution.py:274
  36.0 12.3 %collective-permute-start.10 = (bf16[128,512]{1,0:T(8,128)(2,1)S(1)}, bf16[128,512]{1,0:T(8,128)(2,1)S(1)}, u32[]{:S(2)}, u32[]{:S(2)}) collective-permute-start(bf16[128,512]{1,0:T(8,128)(2,1)S(1)} %get-tuple-element.25), channel_id=1, source_target_pairs={{0,12},{4,0},{8,4},{12,8},{1,13},{5,1},{9,5},{13,9},{2,14},{6,2},{... | collective-permute-start | bytes 393224 | tf_op jit(solution)/shard_map/ppermute | solution.py:274
  38.0 10.3 %collective-permute-start.11 = (bf16[128,512]{1,0:T(8,128)(2,1)S(1)}, bf16[128,512]{1,0:T(8,128)(2,1)S(1)}, u32[]{:S(2)}, u32[]{:S(2)}) collective-permute-start(bf16[128,512]{1,0:T(8,128)(2,1)S(1)} %get-tuple-element.26), channel_id=1, source_target_pairs={{0,4},{4,8},{8,12},{12,0},{1,5},{5,9},{9,13},{13,1},{2,6},{6,10},{... | collective-permute-start | bytes 393224 | tf_op jit(solution)/shard_map/ppermute | solution.py:274
  39.0 18.6 %all-to-all-start = ((bf16[8,128,256]{2,1,0:T(8,128)(2,1)}), bf16[8,128,256]{2,1,0:T(8,128)(2,1)S(1)}, u32[]{:S(2)}, u32[]{:S(2)}) async-start(bf16[8,128,256]{2,1,0:T(8,128)(2,1)} %add_convert_fusion), calls=%async_computation | async-start | bytes 1048576 | tf_op jit(solution)/shard_map/all_to_all | solution.py:296

commit v2 on v1

--- a/solution.py
+++ b/solution.py
@@ -122,10 +122,10 @@
 
     kv_sets = (((0, 0), kv00), ((1, 0), kv10), ((0, 1), kv01), ((1, 1), kv11))
     for (dy, dc), ref in kv_sets:
-        for step in range(GROUPS):
+        for index, step in enumerate((0, 2, 1, 3)):
             for half in range(2):
                 base = pl.multiple_of(start_of(step, dy, dc, half) * HALF, HALF)
-                block = ref[step, half * HALF : (half + 1) * HALF]
+                block = ref[index, half * HALF : (half + 1) * HALF]
                 ks[pl.ds(base, HALF), :] = block[:, :HEAD]
                 vs[pl.ds(base, HALF), :] = block[:, HEAD:]
     for tile in range(SEQ // TILE):
@@ -280,7 +280,8 @@
 
 def on_device(queries, keys, values, out_grad, spans):
     kv0, kv1, kv2, kv3 = cut_kv(keys, values)
-    kv_mine = jnp.stack([kv0, ahead(kv1, 1), ahead(kv2, 2), ahead(kv3, 3)])
+    g2 = ahead(kv2, 2)
+    kv_mine = jnp.stack([kv0, g2, ahead(kv1, 1), ahead(kv3, 3)])
     rows1, rows2, rows3 = cut_rows(queries, out_grad)
     r2 = ahead(rows2, 2)
     r1, r3 = ahead(rows1, 1), ahead(rows3, 3)

time: 58.3 us -> 58 us (level)
  the two profiles are of different devices: /device:TPU:64 before, /device:TPU:160 now
where the time goes in v2:
time: 58 us; the launch traced here: 57 us
  starting transfers between devices  22.8 us (39%)
  waiting for transfers between devices  17.7 us (31%)
  Pallas kernels  9.97 us (17%)
  local copies, waits for them, and re-layouts  4.67 us (8%)
  other arithmetic  1.1 us (2%)
  between operations  0.79 us (1%)
    ppermute x9, starting transfers between devices, ahead(): lax.ppermute(block, 'x', [(i, (i + step) % GROUPS) for i in range(GROUPS)])  11.8 us
    pallas_call x1, Pallas kernels, attention(): pl.pallas_call(attention_kernel, out_shape=[struct((TOK, WIDE), BF16)] *...  9.01 us
    all_to_all x1, waiting for transfers between devices, on_device(): home = lax.all_to_all(total, ('x', 'y'), 0, 0, tiled=True)  7.83 us
    ppermute x9, waiting for transfers between devices, ahead(): lax.ppermute(block, 'x', [(i, (i + step) % GROUPS) for i in range(GROUPS)])  7.49 us
    all_to_all x1, starting transfers between devices, on_device(): home = lax.all_to_all(total, ('x', 'y'), 0, 0, tiled=True)  6.31 us
    ppermute x4, starting transfers between devices, swap(): return lax.ppermute(block, axis, [(0, 1), (1, 0)])  4.76 us
    unnamed x15, local copies, waits for them, and re-layouts  3.94 us
    ppermute x4, waiting for transfers between devices, swap(): return lax.ppermute(block, axis, [(0, 1), (1, 0)])  2.34 us
  transfers between devices with their start and end apart: 14, of which 5 were waited for; matrix products, arithmetic and copies ran while one was open for 2% of the time, Pallas kernels for 2%

profile of v2, /device:TPU:160, one launch (start us, length us, event | category | flops | bytes accessed | tf_op | source)
XLA Modules:
  0.0 57.0 jit_solution(1669982208585494596)
XLA Ops:
  0.6 0.0 copy-start.4
  0.6 0.9 %copy-done.4 = bf16[128,512]{1,0:T(8,128)(2,1)S(1)} copy-done((bf16[128,512]{1,0:T(8,128)(2,1)S(1)}, bf16[128,512]{1,0:T(8,128)(2,1)}, u32[]{:S(2)}) %copy-start.4) | copy-done | bytes 131096
  1.5 0.0 copy-start.5
  1.5 0.9 %copy-done.5 = bf16[128,512]{1,0:T(8,128)(2,1)S(1)} copy-done((bf16[128,512]{1,0:T(8,128)(2,1)S(1)}, bf16[128,512]{1,0:T(8,128)(2,1)}, u32[]{:S(2)}) %copy-start.5) | copy-done | bytes 131096
  2.5 3.1 %collective-permute-start.3 = (bf16[128,256]{1,0:T(8,128)(2,1)S(1)}, bf16[128,256]{1,0:T(8,128)(2,1)S(1)}, u32[]{:S(2)}, u32[]{:S(2)}) collective-permute-start(bf16[128,256]{1,0:T(8,128)(2,1)S(1)} %get-tuple-element.20), channel_id=1, source_target_pairs={{0,8},{4,12},{8,0},{12,4},{1,9},{5,13},{9,1},{13,5},{2,10},{6,14},... | collective-permute-start | bytes 196616 | tf_op jit(solution)/shard_map/ppermute | solution.py:274
  5.6 0.6 %collective-permute-start.4 = (bf16[128,256]{1,0:T(8,128)(2,1)S(1)}, bf16[128,256]{1,0:T(8,128)(2,1)S(1)}, u32[]{:S(2)}, u32[]{:S(2)}) collective-permute-start(bf16[128,256]{1,0:T(8,128)(2,1)S(1)} %get-tuple-element.21), channel_id=1, source_target_pairs={{0,4},{4,8},{8,12},{12,0},{1,5},{5,9},{9,13},{13,1},{2,6},{6,10},{... | collective-permute-start | bytes 196616 | tf_op jit(solution)/shard_map/ppermute | solution.py:274
  6.2 2.6 %collective-permute-start.5 = (bf16[128,256]{1,0:T(8,128)(2,1)S(1)}, bf16[128,256]{1,0:T(8,128)(2,1)S(1)}, u32[]{:S(2)}, u32[]{:S(2)}) collective-permute-start(bf16[128,256]{1,0:T(8,128)(2,1)S(1)} %get-tuple-element.22), channel_id=1, source_target_pairs={{0,12},{4,0},{8,4},{12,8},{1,13},{5,1},{9,5},{13,9},{2,14},{6,2},{... | collective-permute-start | bytes 196616 | tf_op jit(solution)/shard_map/ppermute | solution.py:274
  8.8 0.0 copy-start
  8.8 1.0 %copy-done = bf16[128,2048]{1,0:T(8,128)(2,1)S(1)} copy-done((bf16[128,2048]{1,0:T(8,128)(2,1)S(1)}, bf16[128,2048]{1,0:T(8,128)(2,1)}, u32[]{:S(2)}) %copy-start) | copy-done | bytes 524312
  9.9 0.0 copy-start.2
  9.9 1.0 %copy-done.2 = bf16[128,2048]{1,0:T(8,128)(2,1)S(1)} copy-done((bf16[128,2048]{1,0:T(8,128)(2,1)S(1)}, bf16[128,2048]{1,0:T(8,128)(2,1)}, u32[]{:S(2)}) %copy-start.2) | copy-done | bytes 524312
  10.9 0.1 cut_rows.1
  11.0 0.1 collective-permute-start
  11.1 0.0 collective-permute-done.3
  11.1 0.0 collective-permute-done.4
  11.1 0.0 collective-permute-done.5
  11.2 1.7 %collective-permute-start.6 = (bf16[4,128,256]{2,1,0:T(8,128)(2,1)S(1)}, bf16[4,128,256]{2,1,0:T(8,128)(2,1)S(1)}, u32[]{:S(2)}, u32[]{:S(2)}) collective-permute-start(bf16[4,128,256]{2,1,0:T(8,128)(2,1)S(1)} %pad_maximum_fusion.kv00), channel_id=1, source_target_pairs={{0,2},{2,0},{1,3},{3,1},{4,6},{6,4},{5,7},{7,5},{8,10},{10,8},{9,1... | collective-permute-start | bytes 786440 | tf_op jit(solution)/shard_map/ppermute | solution.py:278
  12.8 0.8 %collective-permute-start.1 = (bf16[128,1024]{1,0:T(8,128)(2,1)S(1)}, bf16[128,1024]{1,0:T(8,128)(2,1)S(1)}, u32[]{:S(2)}, u32[]{:S(2)}) collective-permute-start(bf16[128,1024]{1,0:T(8,128)(2,1)S(1)} %get-tuple-element.17), channel_id=1, source_target_pairs={{0,4},{4,8},{8,12},{12,0},{1,5},{5,9},{9,13},{13,1},{2,6},{6,10},{... | collective-permute-start | bytes 786440 | tf_op jit(solution)/shard_map/ppermute | solution.py:274
  13.7 0.0 copy-start.1
  13.7 0.0 copy-start.3
  13.7 0.0 copy-start.6
  13.7 2.5 %collective-permute-start.2 = (bf16[128,1024]{1,0:T(8,128)(2,1)S(1)}, bf16[128,1024]{1,0:T(8,128)(2,1)S(1)}, u32[]{:S(2)}, u32[]{:S(2)}) collective-permute-start(bf16[128,1024]{1,0:T(8,128)(2,1)S(1)} %get-tuple-element.18), channel_id=1, source_target_pairs={{0,12},{4,0},{8,4},{12,8},{1,13},{5,1},{9,5},{13,9},{2,14},{6,2},{... | collective-permute-start | bytes 786440 | tf_op jit(solution)/shard_map/ppermute | solution.py:274
  16.1 0.0 collective-permute-start.7
  16.1 2.3 %collective-permute-done.6.kv10 = bf16[4,128,256]{2,1,0:T(8,128)(2,1)S(1)} collective-permute-done((bf16[4,128,256]{2,1,0:T(8,128)(2,1)S(1)}, bf16[4,128,256]{2,1,0:T(8,128)(2,1)S(1)}, u32[]{:S(2)}, u32[]{:S(2)}) %collective-permute-start.6) | collective-permute-done | bytes 262176 | tf_op jit(solution)/shard_map/ppermute | solution.py:278
  18.5 0.0 collective-permute-start.8
  18.5 3.4 %collective-permute-done.r1.r2 = bf16[128,1024]{1,0:T(8,128)(2,1)S(1)} collective-permute-done((bf16[128,1024]{1,0:T(8,128)(2,1)S(1)}, bf16[128,1024]{1,0:T(8,128)(2,1)S(1)}, u32[]{:S(2)}, u32[]{:S(2)}) %collective-permute-start) | collective-permute-done | bytes 262176 | tf_op jit(solution)/shard_map/ppermute | solution.py:274
  21.9 3.5 %collective-permute-done.1.r2.r1 = bf16[128,1024]{1,0:T(8,128)(2,1)S(1)} collective-permute-done((bf16[128,1024]{1,0:T(8,128)(2,1)S(1)}, bf16[128,1024]{1,0:T(8,128)(2,1)S(1)}, u32[]{:S(2)}, u32[]{:S(2)}) %collective-permute-start.1) | collective-permute-done | bytes 262176 | tf_op jit(solution)/shard_map/ppermute | solution.py:274
  25.4 0.0 collective-permute-done.2.r3
  25.4 0.0 collective-permute-done.7.kv01
  25.4 0.0 collective-permute-done.8.kv11
  25.4 0.0 copy-done.1
  25.4 0.0 copy-done.3
  25.5 0.0 copy-done.6
  25.5 9.0 %attention_backward.1 = (bf16[128,512]{1,0:T(8,128)(2,1)S(1)}, bf16[128,512]{1,0:T(8,128)(2,1)S(1)}, bf16[128,512]{1,0:T(8,128)(2,1)S(1)}, bf16[128,512]{1,0:T(8...) custom-call(s32[32]{0:T(128)S(1)} %copy-done.6, bf16[8,128]{1,0:T(8,128)(2,1)S(1)} %rows_arrived.1.token, ...), custom_call_target="tpu_custom_call" | custom-call | tf_op jit(solution)/shard_map/attention_backward/pallas_call | solution.py:218
  34.5 3.1 %collective-permute-start.12 = (bf16[8,128,256]{2,1,0:T(8,128)(2,1)S(1)}, bf16[8,128,256]{2,1,0:T(8,128)(2,1)S(1)}, u32[]{:S(2)}, u32[]{:S(2)}) collective-permute-start(bf16[8,128,256]{2,1,0:T(8,128)(2,1)S(1)} %get-tuple-element.28), channel_id=1, source_target_pairs={{0,1},{1,0},{2,3},{3,2},{4,5},{5,4},{6,7},{7,6},{8,9},{9,8},{10,11... | collective-permute-start | bytes 1572872 | tf_op jit(solution)/shard_map/ppermute | solution.py:278
  37.6 0.0 collective-permute-start.9
  37.6 0.7 %collective-permute-start.10 = (bf16[128,512]{1,0:T(8,128)(2,1)S(1)}, bf16[128,512]{1,0:T(8,128)(2,1)S(1)}, u32[]{:S(2)}, u32[]{:S(2)}) collective-permute-start(bf16[128,512]{1,0:T(8,128)(2,1)S(1)} %get-tuple-element.25), channel_id=1, source_target_pairs={{0,12},{4,0},{8,4},{12,8},{1,13},{5,1},{9,5},{13,9},{2,14},{6,2},{... | collective-permute-start | bytes 393224 | tf_op jit(solution)/shard_map/ppermute | solution.py:274
  38.3 1.3 %collective-permute-start.11 = (bf16[128,512]{1,0:T(8,128)(2,1)S(1)}, bf16[128,512]{1,0:T(8,128)(2,1)S(1)}, u32[]{:S(2)}, u32[]{:S(2)}) collective-permute-start(bf16[128,512]{1,0:T(8,128)(2,1)S(1)} %get-tuple-element.26), channel_id=1, source_target_pairs={{0,4},{4,8},{8,12},{12,0},{1,5},{5,9},{9,13},{13,1},{2,6},{6,10},{... | collective-permute-start | bytes 393224 | tf_op jit(solution)/shard_map/ppermute | solution.py:274
  39.6 0.0 collective-permute-done.12
  39.6 0.9 %add_convert_fusion = bf16[8,128,256]{2,1,0:T(8,128)(2,1)} fusion(f32[8,128,256]{2,1,0:T(8,128)S(1)} %get-tuple-element.27, bf16[8,128,256]{2,1,0:T(8,128)(2,1)S(1)} %collective-permute-done.12), kind=kLoop, calls=%fused_computation | loop fusion | flops 786432 | bytes 2097152 | tf_op jit(solution)/shard_map/convert_element_type | solution.py:296
  40.5 6.3 %all-to-all-start = ((bf16[8,128,256]{2,1,0:T(8,128)(2,1)}), bf16[8,128,256]{2,1,0:T(8,128)(2,1)S(1)}, u32[]{:S(2)}, u32[]{:S(2)}) async-start(bf16[8,128,256]{2,1,0:T(8,128)(2,1)} %add_convert_fusion), calls=%async_computation | async-start | bytes 1048576 | tf_op jit(solution)/shard_map/all_to_all | solution.py:297
  46.8 0.0 collective-permute-done.9.p2
  46.8 0.0 collective-permute-done.10.p1
  46.9 0.5 collective-permute-done.11.p3
  47.4 0.9 %join_rows.1 = bf16[128,2048]{1,0:T(8,128)(2,1)} custom-call(bf16[128,512]{1,0:T(8,128)(2,1)S(1)} %get-tuple-element.23.p0, bf16[128,512]{1,0:T(8,128)(2,1)S(1)} %collective-permute-done.9.p2, bf16[128,512]{1,0:T(8,128)(2,1)S(1)} %collective-permute-done.10.p1, bf16[128,512]{1,0:T(8,128)(2,1)S(1)} %collective-permute-done.11.p3), custom_call_target="tpu_custom_call" | custom-call | flops 30000001024 | bytes 60000000 | tf_op jit(solution)/shard_map/join_rows/pallas_call | solution.py:254
  48.2 7.8 %all-to-all-done = bf16[8,128,256]{2,1,0:T(8,128)(2,1)S(1)} async-done(((bf16[8,128,256]{2,1,0:T(8,128)(2,1)}), bf16[8,128,256]{2,1,0:T(8,128)(2,1)S(1)}, u32[]{:S(2)}, u32[]{:S(2)}) %all-to-all-start) | async-done | bytes 524320 | tf_op jit(solution)/shard_map/all_to_all | solution.py:297
  56.1 0.1 convert.1
  56.2 0.1 fusion.1
  56.3 0.7 %copy_bitcast_fusion = (bf16[128,512]{1,0:T(8,128)(2,1)}, bf16[128,512]{1,0:T(8,128)(2,1)}) fusion(bf16[4,16,8,128]{3,2,1,0:T(8,128)(2,1)S(1)} %get-tuple-element.29, bf16[4,16,8,128]{3,2,1,0:T(8,128)(2,1)S(1)} %get-tuple-element.30), kind=kLoop, calls=%fused_computation.5 | loop fusion | bytes 524288 | tf_op jit(solution)/shard_map/reshape | solution.py:269
  (4 shorter events, 0.1 us)
Async XLA Ops:
  0.6 0.9 %copy-start.4 = (bf16[128,512]{1,0:T(8,128)(2,1)S(1)}, bf16[128,512]{1,0:T(8,128)(2,1)}, u32[]{:S(2)}) copy-start(bf16[128,512]{1,0:T(8,128)(2,1)} %keys.1) | copy-start | bytes 393220
  1.5 0.9 %copy-start.5 = (bf16[128,512]{1,0:T(8,128)(2,1)S(1)}, bf16[128,512]{1,0:T(8,128)(2,1)}, u32[]{:S(2)}) copy-start(bf16[128,512]{1,0:T(8,128)(2,1)} %values.1) | copy-start | bytes 393220
  2.5 8.6 %collective-permute-start.3 = (bf16[128,256]{1,0:T(8,128)(2,1)S(1)}, bf16[128,256]{1,0:T(8,128)(2,1)S(1)}, u32[]{:S(2)}, u32[]{:S(2)}) collective-permute-start(bf16[128,256]{1,0:T(8,128)(2,1)S(1)} %get-tuple-element.20), channel_id=1, source_target_pairs={{0,8},{4,12},{8,0},{12,4},{1,9},{5,13},{9,1},{13,5},{2,10},{6,14},... | collective-permute-start | bytes 196616 | tf_op jit(solution)/shard_map/ppermute | solution.py:274
  5.6 5.5 %collective-permute-start.4 = (bf16[128,256]{1,0:T(8,128)(2,1)S(1)}, bf16[128,256]{1,0:T(8,128)(2,1)S(1)}, u32[]{:S(2)}, u32[]{:S(2)}) collective-permute-start(bf16[128,256]{1,0:T(8,128)(2,1)S(1)} %get-tuple-element.21), channel_id=1, source_target_pairs={{0,4},{4,8},{8,12},{12,0},{1,5},{5,9},{9,13},{13,1},{2,6},{6,10},{... | collective-permute-start | bytes 196616 | tf_op jit(solution)/shard_map/ppermute | solution.py:274
  6.2 4.9 %collective-permute-start.5 = (bf16[128,256]{1,0:T(8,128)(2,1)S(1)}, bf16[128,256]{1,0:T(8,128)(2,1)S(1)}, u32[]{:S(2)}, u32[]{:S(2)}) collective-permute-start(bf16[128,256]{1,0:T(8,128)(2,1)S(1)} %get-tuple-element.22), channel_id=1, source_target_pairs={{0,12},{4,0},{8,4},{12,8},{1,13},{5,1},{9,5},{13,9},{2,14},{6,2},{... | collective-permute-start | bytes 196616 | tf_op jit(solution)/shard_map/ppermute | solution.py:274
  8.8 1.0 %copy-start = (bf16[128,2048]{1,0:T(8,128)(2,1)S(1)}, bf16[128,2048]{1,0:T(8,128)(2,1)}, u32[]{:S(2)}) copy-start(bf16[128,2048]{1,0:T(8,128)(2,1)} %queries.3) | copy-start | bytes 1572868
  9.9 1.0 %copy-start.2 = (bf16[128,2048]{1,0:T(8,128)(2,1)S(1)}, bf16[128,2048]{1,0:T(8,128)(2,1)}, u32[]{:S(2)}) copy-start(bf16[128,2048]{1,0:T(8,128)(2,1)} %out_grad.3) | copy-start | bytes 1572868
  11.0 10.9 %collective-permute-start = (bf16[128,1024]{1,0:T(8,128)(2,1)S(1)}, bf16[128,1024]{1,0:T(8,128)(2,1)S(1)}, u32[]{:S(2)}, u32[]{:S(2)}) collective-permute-start(bf16[128,1024]{1,0:T(8,128)(2,1)S(1)} %get-tuple-element.16), channel_id=1, source_target_pairs={{0,8},{4,12},{8,0},{12,4},{1,9},{5,13},{9,1},{13,5},{2,10},{6,14},... | collective-permute-start | bytes 786440 | tf_op jit(solution)/shard_map/ppermute | solution.py:274
  11.2 7.3 %collective-permute-start.6 = (bf16[4,128,256]{2,1,0:T(8,128)(2,1)S(1)}, bf16[4,128,256]{2,1,0:T(8,128)(2,1)S(1)}, u32[]{:S(2)}, u32[]{:S(2)}) collective-permute-start(bf16[4,128,256]{2,1,0:T(8,128)(2,1)S(1)} %pad_maximum_fusion.kv00), channel_id=1, source_target_pairs={{0,2},{2,0},{1,3},{3,1},{4,6},{6,4},{5,7},{7,5},{8,10},{10,8},{9,1... | collective-permute-start | bytes 786440 | tf_op jit(solution)/shard_map/ppermute | solution.py:278
  12.8 12.6 %collective-permute-start.1 = (bf16[128,1024]{1,0:T(8,128)(2,1)S(1)}, bf16[128,1024]{1,0:T(8,128)(2,1)S(1)}, u32[]{:S(2)}, u32[]{:S(2)}) collective-permute-start(bf16[128,1024]{1,0:T(8,128)(2,1)S(1)} %get-tuple-element.17), channel_id=1, source_target_pairs={{0,4},{4,8},{8,12},{12,0},{1,5},{5,9},{9,13},{13,1},{2,6},{6,10},{... | collective-permute-start | bytes 786440 | tf_op jit(solution)/shard_map/ppermute | solution.py:274
  13.7 11.8 %copy-start.1 = (bf16[128,2048]{1,0:T(8,128)(2,1)S(1)}, bf16[128,2048]{1,0:T(8,128)(2,1)}, u32[]{:S(2)}) copy-start(bf16[128,2048]{1,0:T(8,128)(2,1)} %queries.3) | copy-start | bytes 1572868
  13.7 11.8 %copy-start.3 = (bf16[128,2048]{1,0:T(8,128)(2,1)S(1)}, bf16[128,2048]{1,0:T(8,128)(2,1)}, u32[]{:S(2)}) copy-start(bf16[128,2048]{1,0:T(8,128)(2,1)} %out_grad.3) | copy-start | bytes 1572868
  13.7 11.8 %copy-start.6 = (s32[32]{0:T(128)S(1)}, s32[32]{0:T(128)}, u32[]{:S(2)}) copy-start(s32[32]{0:T(128)} %spans.1) | copy-start | bytes 388
  13.7 11.7 %collective-permute-start.2 = (bf16[128,1024]{1,0:T(8,128)(2,1)S(1)}, bf16[128,1024]{1,0:T(8,128)(2,1)S(1)}, u32[]{:S(2)}, u32[]{:S(2)}) collective-permute-start(bf16[128,1024]{1,0:T(8,128)(2,1)S(1)} %get-tuple-element.18), channel_id=1, source_target_pairs={{0,12},{4,0},{8,4},{12,8},{1,13},{5,1},{9,5},{13,9},{2,14},{6,2},{... | collective-permute-start | bytes 786440 | tf_op jit(solution)/shard_map/ppermute | solution.py:274
  16.1 9.3 %collective-permute-start.7 = (bf16[4,128,256]{2,1,0:T(8,128)(2,1)S(1)}, bf16[4,128,256]{2,1,0:T(8,128)(2,1)S(1)}, u32[]{:S(2)}, u32[]{:S(2)}) collective-permute-start(bf16[4,128,256]{2,1,0:T(8,128)(2,1)S(1)} %pad_maximum_fusion.kv00), channel_id=1, source_target_pairs={{0,1},{1,0},{2,3},{3,2},{4,5},{5,4},{6,7},{7,6},{8,9},{9,8},{10,11... | collective-permute-start | bytes 786440 | tf_op jit(solution)/shard_map/ppermute | solution.py:278
  18.5 7.0 %collective-permute-start.8 = (bf16[4,128,256]{2,1,0:T(8,128)(2,1)S(1)}, bf16[4,128,256]{2,1,0:T(8,128)(2,1)S(1)}, u32[]{:S(2)}, u32[]{:S(2)}) collective-permute-start(bf16[4,128,256]{2,1,0:T(8,128)(2,1)S(1)} %collective-permute-done.6.kv10), channel_id=1, source_target_pairs={{0,1},{1,0},{2,3},{3,2},{4,5},{5,4},{6,7},{7,6},{8,9},{9,8},{10,11... | collective-permute-start | bytes 786440 | tf_op jit(solution)/shard_map/ppermute | solution.py:278
  34.5 5.1 %collective-permute-start.12 = (bf16[8,128,256]{2,1,0:T(8,128)(2,1)S(1)}, bf16[8,128,256]{2,1,0:T(8,128)(2,1)S(1)}, u32[]{:S(2)}, u32[]{:S(2)}) collective-permute-start(bf16[8,128,256]{2,1,0:T(8,128)(2,1)S(1)} %get-tuple-element.28), channel_id=1, source_target_pairs={{0,1},{1,0},{2,3},{3,2},{4,5},{5,4},{6,7},{7,6},{8,9},{9,8},{10,11... | collective-permute-start | bytes 1572872 | tf_op jit(solution)/shard_map/ppermute | solution.py:278
  37.6 9.3 %collective-permute-start.9 = (bf16[128,512]{1,0:T(8,128)(2,1)S(1)}, bf16[128,512]{1,0:T(8,128)(2,1)S(1)}, u32[]{:S(2)}, u32[]{:S(2)}) collective-permute-start(bf16[128,512]{1,0:T(8,128)(2,1)S(1)} %get-tuple-element.24), channel_id=1, source_target_pairs={{0,8},{4,12},{8,0},{12,4},{1,9},{5,13},{9,1},{13,5},{2,10},{6,14},... | collective-permute-start | bytes 393224 | tf_op jit(solution)/shard_map/ppermute | solution.py:274
  37.6 9.3 %collective-permute-start.10 = (bf16[128,512]{1,0:T(8,128)(2,1)S(1)}, bf16[128,512]{1,0:T(8,128)(2,1)S(1)}, u32[]{:S(2)}, u32[]{:S(2)}) collective-permute-start(bf16[128,512]{1,0:T(8,128)(2,1)S(1)} %get-tuple-element.25), channel_id=1, source_target_pairs={{0,12},{4,0},{8,4},{12,8},{1,13},{5,1},{9,5},{13,9},{2,14},{6,2},{... | collective-permute-start | bytes 393224 | tf_op jit(solution)/shard_map/ppermute | solution.py:274
  38.3 9.1 %collective-permute-start.11 = (bf16[128,512]{1,0:T(8,128)(2,1)S(1)}, bf16[128,512]{1,0:T(8,128)(2,1)S(1)}, u32[]{:S(2)}, u32[]{:S(2)}) collective-permute-start(bf16[128,512]{1,0:T(8,128)(2,1)S(1)} %get-tuple-element.26), channel_id=1, source_target_pairs={{0,4},{4,8},{8,12},{12,0},{1,5},{5,9},{9,13},{13,1},{2,6},{6,10},{... | collective-permute-start | bytes 393224 | tf_op jit(solution)/shard_map/ppermute | solution.py:274
  40.5 15.5 %all-to-all-start = ((bf16[8,128,256]{2,1,0:T(8,128)(2,1)}), bf16[8,128,256]{2,1,0:T(8,128)(2,1)S(1)}, u32[]{:S(2)}, u32[]{:S(2)}) async-start(bf16[8,128,256]{2,1,0:T(8,128)(2,1)} %add_convert_fusion), calls=%async_computation | async-start | bytes 1048576 | tf_op jit(solution)/shard_map/all_to_all | solution.py:297

commit v3 on v2

--- a/solution.py
+++ b/solution.py
@@ -219,7 +219,7 @@
         attention_kernel,
         out_shape=[struct((TOK, WIDE), BF16)] * GROUPS
         + [
-            struct((2 * GROUPS, TOK, 2 * HEAD), F32),
+            struct((2 * GROUPS, TOK, 2 * HEAD), BF16),
             struct((2 * GROUPS, TOK, 2 * HEAD), BF16),
         ],
         in_specs=[SMEM, VMEM, ANY, ANY] + [VMEM] * 7,
@@ -293,7 +293,7 @@
     dq0, dq1, dq2, dq3, keep, send = attention(
         spans, token, queries, out_grad, row_pieces, [kv_mine, kv_y, kv_c, kv_yc]
     )
-    total = (keep + swap(send, "c").astype(F32)).astype(BF16)
+    total = (keep.astype(F32) + swap(send, "c").astype(F32)).astype(BF16)
     home = lax.all_to_all(total, ("x", "y"), 0, 0, tiled=True)
     home2 = ahead(dq2, 2)
     home1, home3 = ahead(dq1, 3), ahead(dq3, 1)

time: 58 us -> 58.2 us (level)
  Pallas kernels: 9.97 us -> 11.5 us
    ppermute x4, starting transfers between devices: 4.76 us -> 1.79 us  [swap(): return lax.ppermute(block, axis, [(0, 1), (1, 0)])]
    all_to_all x1, starting transfers between devices: 6.31 us -> 8.49 us  [on_device(): home = lax.all_to_all(total, ('x', 'y'), 0, 0, tiled=True)]
    pallas_call x1, Pallas kernels: 9.01 us -> 10.5 us  [attention(): pl.pallas_call(attention_kernel, out_shape=[struct((TOK, WIDE), BF16)] *...]
  transfers between devices with their start and end apart: 14 -> 14, of which waited for: 5 -> 4; matrix products, arithmetic and copies ran while one was open for 2% -> 2% of each run, Pallas kernels for 2% -> 2%
where the time goes in v3:
time: 58.2 us; the launch traced here: 57.7 us
  starting transfers between devices  22.4 us (38%)
  waiting for transfers between devices  17.3 us (30%)
  Pallas kernels  11.5 us (20%)
  local copies, waits for them, and re-layouts  4.67 us (8%)
  other arithmetic  1.12 us (2%)
  between operations  0.79 us (1%)
    ppermute x9, starting transfers between devices, ahead(): lax.ppermute(block, 'x', [(i, (i + step) % GROUPS) for i in range(GROUPS)])  12.1 us
    pallas_call x1, Pallas kernels, attention(): pl.pallas_call(attention_kernel, out_shape=[struct((TOK, WIDE), BF16)] *...  10.5 us
    all_to_all x1, starting transfers between devices, on_device(): home = lax.all_to_all(total, ('x', 'y'), 0, 0, tiled=True)  8.49 us
    all_to_all x1, waiting for transfers between devices, on_device(): home = lax.all_to_all(total, ('x', 'y'), 0, 0, tiled=True)  8.01 us
    ppermute x9, waiting for transfers between devices, ahead(): lax.ppermute(block, 'x', [(i, (i + step) % GROUPS) for i in range(GROUPS)])  6.96 us
    unnamed x15, local copies, waits for them, and re-layouts  3.94 us
    ppermute x4, waiting for transfers between devices, swap(): return lax.ppermute(block, axis, [(0, 1), (1, 0)])  2.34 us
    ppermute x4, starting transfers between devices, swap(): return lax.ppermute(block, axis, [(0, 1), (1, 0)])  1.79 us
  transfers between devices with their start and end apart: 14, of which 4 were waited for; matrix products, arithmetic and copies ran while one was open for 2% of the time, Pallas kernels for 2%

profile of v3, /device:TPU:160, one launch (start us, length us, event | category | flops | bytes accessed | tf_op | source)
XLA Modules:
  0.0 57.7 jit_solution(13456062651147730713)
XLA Ops:
  0.6 0.0 copy-start.4
  0.6 0.9 %copy-done.4 = bf16[128,512]{1,0:T(8,128)(2,1)S(1)} copy-done((bf16[128,512]{1,0:T(8,128)(2,1)S(1)}, bf16[128,512]{1,0:T(8,128)(2,1)}, u32[]{:S(2)}) %copy-start.4) | copy-done | bytes 131096
  1.5 0.0 copy-start.5
  1.5 0.9 %copy-done.5 = bf16[128,512]{1,0:T(8,128)(2,1)S(1)} copy-done((bf16[128,512]{1,0:T(8,128)(2,1)S(1)}, bf16[128,512]{1,0:T(8,128)(2,1)}, u32[]{:S(2)}) %copy-start.5) | copy-done | bytes 131096
  2.5 3.1 %collective-permute-start.3 = (bf16[128,256]{1,0:T(8,128)(2,1)S(1)}, bf16[128,256]{1,0:T(8,128)(2,1)S(1)}, u32[]{:S(2)}, u32[]{:S(2)}) collective-permute-start(bf16[128,256]{1,0:T(8,128)(2,1)S(1)} %get-tuple-element.20), channel_id=1, source_target_pairs={{0,8},{4,12},{8,0},{12,4},{1,9},{5,13},{9,1},{13,5},{2,10},{6,14},... | collective-permute-start | bytes 196616 | tf_op jit(solution)/shard_map/ppermute | solution.py:274
  5.6 0.6 %collective-permute-start.4 = (bf16[128,256]{1,0:T(8,128)(2,1)S(1)}, bf16[128,256]{1,0:T(8,128)(2,1)S(1)}, u32[]{:S(2)}, u32[]{:S(2)}) collective-permute-start(bf16[128,256]{1,0:T(8,128)(2,1)S(1)} %get-tuple-element.21), channel_id=1, source_target_pairs={{0,4},{4,8},{8,12},{12,0},{1,5},{5,9},{9,13},{13,1},{2,6},{6,10},{... | collective-permute-start | bytes 196616 | tf_op jit(solution)/shard_map/ppermute | solution.py:274
  6.2 2.6 %collective-permute-start.5 = (bf16[128,256]{1,0:T(8,128)(2,1)S(1)}, bf16[128,256]{1,0:T(8,128)(2,1)S(1)}, u32[]{:S(2)}, u32[]{:S(2)}) collective-permute-start(bf16[128,256]{1,0:T(8,128)(2,1)S(1)} %get-tuple-element.22), channel_id=1, source_target_pairs={{0,12},{4,0},{8,4},{12,8},{1,13},{5,1},{9,5},{13,9},{2,14},{6,2},{... | collective-permute-start | bytes 196616 | tf_op jit(solution)/shard_map/ppermute | solution.py:274
  8.8 0.0 copy-start
  8.8 1.0 %copy-done = bf16[128,2048]{1,0:T(8,128)(2,1)S(1)} copy-done((bf16[128,2048]{1,0:T(8,128)(2,1)S(1)}, bf16[128,2048]{1,0:T(8,128)(2,1)}, u32[]{:S(2)}) %copy-start) | copy-done | bytes 524312
  9.9 0.0 copy-start.2
  9.9 1.0 %copy-done.2 = bf16[128,2048]{1,0:T(8,128)(2,1)S(1)} copy-done((bf16[128,2048]{1,0:T(8,128)(2,1)S(1)}, bf16[128,2048]{1,0:T(8,128)(2,1)}, u32[]{:S(2)}) %copy-start.2) | copy-done | bytes 524312
  10.9 0.1 cut_rows.1
  11.0 0.1 collective-permute-start
  11.1 0.0 collective-permute-done.3
  11.1 0.0 collective-permute-done.4
  11.1 0.0 collective-permute-done.5
  11.2 1.7 %collective-permute-start.6 = (bf16[4,128,256]{2,1,0:T(8,128)(2,1)S(1)}, bf16[4,128,256]{2,1,0:T(8,128)(2,1)S(1)}, u32[]{:S(2)}, u32[]{:S(2)}) collective-permute-start(bf16[4,128,256]{2,1,0:T(8,128)(2,1)S(1)} %pad_maximum_fusion.kv00), channel_id=1, source_target_pairs={{0,2},{2,0},{1,3},{3,1},{4,6},{6,4},{5,7},{7,5},{8,10},{10,8},{9,1... | collective-permute-start | bytes 786440 | tf_op jit(solution)/shard_map/ppermute | solution.py:278
  12.8 0.8 %collective-permute-start.1 = (bf16[128,1024]{1,0:T(8,128)(2,1)S(1)}, bf16[128,1024]{1,0:T(8,128)(2,1)S(1)}, u32[]{:S(2)}, u32[]{:S(2)}) collective-permute-start(bf16[128,1024]{1,0:T(8,128)(2,1)S(1)} %get-tuple-element.17), channel_id=1, source_target_pairs={{0,4},{4,8},{8,12},{12,0},{1,5},{5,9},{9,13},{13,1},{2,6},{6,10},{... | collective-permute-start | bytes 786440 | tf_op jit(solution)/shard_map/ppermute | solution.py:274
  13.7 0.0 copy-start.1
  13.7 0.0 copy-start.3
  13.7 0.0 copy-start.6
  13.7 2.5 %collective-permute-start.2 = (bf16[128,1024]{1,0:T(8,128)(2,1)S(1)}, bf16[128,1024]{1,0:T(8,128)(2,1)S(1)}, u32[]{:S(2)}, u32[]{:S(2)}) collective-permute-start(bf16[128,1024]{1,0:T(8,128)(2,1)S(1)} %get-tuple-element.18), channel_id=1, source_target_pairs={{0,12},{4,0},{8,4},{12,8},{1,13},{5,1},{9,5},{13,9},{2,14},{6,2},{... | collective-permute-start | bytes 786440 | tf_op jit(solution)/shard_map/ppermute | solution.py:274
  16.1 0.0 collective-permute-start.7
  16.1 2.3 %collective-permute-done.6.kv10 = bf16[4,128,256]{2,1,0:T(8,128)(2,1)S(1)} collective-permute-done((bf16[4,128,256]{2,1,0:T(8,128)(2,1)S(1)}, bf16[4,128,256]{2,1,0:T(8,128)(2,1)S(1)}, u32[]{:S(2)}, u32[]{:S(2)}) %collective-permute-start.6) | collective-permute-done | bytes 262176 | tf_op jit(solution)/shard_map/ppermute | solution.py:278
  18.5 0.0 collective-permute-start.8
  18.5 3.4 %collective-permute-done.r1.r2 = bf16[128,1024]{1,0:T(8,128)(2,1)S(1)} collective-permute-done((bf16[128,1024]{1,0:T(8,128)(2,1)S(1)}, bf16[128,1024]{1,0:T(8,128)(2,1)S(1)}, u32[]{:S(2)}, u32[]{:S(2)}) %collective-permute-start) | collective-permute-done | bytes 262176 | tf_op jit(solution)/shard_map/ppermute | solution.py:274
  21.9 3.5 %collective-permute-done.1.r2.r1 = bf16[128,1024]{1,0:T(8,128)(2,1)S(1)} collective-permute-done((bf16[128,1024]{1,0:T(8,128)(2,1)S(1)}, bf16[128,1024]{1,0:T(8,128)(2,1)S(1)}, u32[]{:S(2)}, u32[]{:S(2)}) %collective-permute-start.1) | collective-permute-done | bytes 262176 | tf_op jit(solution)/shard_map/ppermute | solution.py:274
  25.4 0.0 collective-permute-done.2.r3
  25.4 0.0 collective-permute-done.7.kv01
  25.4 0.0 collective-permute-done.8.kv11
  25.4 0.0 copy-done.1
  25.4 0.0 copy-done.3
  25.4 0.0 copy-done.6
  25.5 10.5 %attention_backward.1 = (bf16[128,512]{1,0:T(8,128)(2,1)S(1)}, bf16[128,512]{1,0:T(8,128)(2,1)S(1)}, bf16[128,512]{1,0:T(8,128)(2,1)S(1)}, bf16[128,512]{1,0:T(8...) custom-call(s32[32]{0:T(128)S(1)} %copy-done.6, ...), custom_call_target="tpu_custom_call" | custom-call | tf_op jit(solution)/shard_map/attention_backward/pallas_call | solution.py:218
  36.0 0.1 collective-permute-start.12
  36.1 0.3 collective-permute-start.9
  36.4 1.8 %collective-permute-start.10 = (bf16[128,512]{1,0:T(8,128)(2,1)S(1)}, bf16[128,512]{1,0:T(8,128)(2,1)S(1)}, u32[]{:S(2)}, u32[]{:S(2)}) collective-permute-start(bf16[128,512]{1,0:T(8,128)(2,1)S(1)} %get-tuple-element.25), channel_id=1, source_target_pairs={{0,12},{4,0},{8,4},{12,8},{1,13},{5,1},{9,5},{13,9},{2,14},{6,2},{... | collective-permute-start | bytes 393224 | tf_op jit(solution)/shard_map/ppermute | solution.py:274
  38.2 0.3 collective-permute-start.11
  38.5 0.0 collective-permute-done.12
  38.5 0.9 %add_convert_fusion = bf16[8,128,256]{2,1,0:T(8,128)(2,1)} fusion(bf16[8,128,256]{2,1,0:T(8,128)(2,1)S(1)} %collective-permute-done.12, bf16[8,128,256]{2,1,0:T(8,128)(2,1)S(1)} %get-tuple-element.27), kind=kLoop, calls=%fused_computation | loop fusion | flops 1048576 | bytes 1572864 | tf_op jit(solution)/shard_map/convert_element_type | solution.py:296
  39.4 8.5 %all-to-all-start = ((bf16[8,128,256]{2,1,0:T(8,128)(2,1)}), bf16[8,128,256]{2,1,0:T(8,128)(2,1)S(1)}, u32[]{:S(2)}, u32[]{:S(2)}) async-start(bf16[8,128,256]{2,1,0:T(8,128)(2,1)} %add_convert_fusion), calls=%async_computation | async-start | bytes 1048576 | tf_op jit(solution)/shard_map/all_to_all | solution.py:297
  47.9 0.0 collective-permute-done.9.p2
  47.9 0.0 collective-permute-done.10.p1
  47.9 0.0 collective-permute-done.11.p3
  47.9 0.9 %join_rows.1 = bf16[128,2048]{1,0:T(8,128)(2,1)} custom-call(bf16[128,512]{1,0:T(8,128)(2,1)S(1)} %get-tuple-element.23.p0, bf16[128,512]{1,0:T(8,128)(2,1)S(1)} %collective-permute-done.9.p2, bf16[128,512]{1,0:T(8,128)(2,1)S(1)} %collective-permute-done.10.p1, bf16[128,512]{1,0:T(8,128)(2,1)S(1)} %collective-permute-done.11.p3), custom_call_target="tpu_custom_call" | custom-call | flops 30000001024 | bytes 60000000 | tf_op jit(solution)/shard_map/join_rows/pallas_call | solution.py:254
  48.8 8.0 %all-to-all-done = bf16[8,128,256]{2,1,0:T(8,128)(2,1)S(1)} async-done(((bf16[8,128,256]{2,1,0:T(8,128)(2,1)}), bf16[8,128,256]{2,1,0:T(8,128)(2,1)S(1)}, u32[]{:S(2)}, u32[]{:S(2)}) %all-to-all-start) | async-done | bytes 524320 | tf_op jit(solution)/shard_map/all_to_all | solution.py:297
  56.8 0.1 convert.1
  56.9 0.1 fusion.1
  57.0 0.7 %copy_bitcast_fusion = (bf16[128,512]{1,0:T(8,128)(2,1)}, bf16[128,512]{1,0:T(8,128)(2,1)}) fusion(bf16[4,16,8,128]{3,2,1,0:T(8,128)(2,1)S(1)} %get-tuple-element.29, bf16[4,16,8,128]{3,2,1,0:T(8,128)(2,1)S(1)} %get-tuple-element.30), kind=kLoop, calls=%fused_computation.5 | loop fusion | bytes 524288 | tf_op jit(solution)/shard_map/reshape | solution.py:269
  (4 shorter events, 0.1 us)
Async XLA Ops:
  0.6 0.9 %copy-start.4 = (bf16[128,512]{1,0:T(8,128)(2,1)S(1)}, bf16[128,512]{1,0:T(8,128)(2,1)}, u32[]{:S(2)}) copy-start(bf16[128,512]{1,0:T(8,128)(2,1)} %keys.1) | copy-start | bytes 393220
  1.5 0.9 %copy-start.5 = (bf16[128,512]{1,0:T(8,128)(2,1)S(1)}, bf16[128,512]{1,0:T(8,128)(2,1)}, u32[]{:S(2)}) copy-start(bf16[128,512]{1,0:T(8,128)(2,1)} %values.1) | copy-start | bytes 393220
  2.5 8.6 %collective-permute-start.3 = (bf16[128,256]{1,0:T(8,128)(2,1)S(1)}, bf16[128,256]{1,0:T(8,128)(2,1)S(1)}, u32[]{:S(2)}, u32[]{:S(2)}) collective-permute-start(bf16[128,256]{1,0:T(8,128)(2,1)S(1)} %get-tuple-element.20), channel_id=1, source_target_pairs={{0,8},{4,12},{8,0},{12,4},{1,9},{5,13},{9,1},{13,5},{2,10},{6,14},... | collective-permute-start | bytes 196616 | tf_op jit(solution)/shard_map/ppermute | solution.py:274
  5.6 5.5 %collective-permute-start.4 = (bf16[128,256]{1,0:T(8,128)(2,1)S(1)}, bf16[128,256]{1,0:T(8,128)(2,1)S(1)}, u32[]{:S(2)}, u32[]{:S(2)}) collective-permute-start(bf16[128,256]{1,0:T(8,128)(2,1)S(1)} %get-tuple-element.21), channel_id=1, source_target_pairs={{0,4},{4,8},{8,12},{12,0},{1,5},{5,9},{9,13},{13,1},{2,6},{6,10},{... | collective-permute-start | bytes 196616 | tf_op jit(solution)/shard_map/ppermute | solution.py:274
  6.2 4.9 %collective-permute-start.5 = (bf16[128,256]{1,0:T(8,128)(2,1)S(1)}, bf16[128,256]{1,0:T(8,128)(2,1)S(1)}, u32[]{:S(2)}, u32[]{:S(2)}) collective-permute-start(bf16[128,256]{1,0:T(8,128)(2,1)S(1)} %get-tuple-element.22), channel_id=1, source_target_pairs={{0,12},{4,0},{8,4},{12,8},{1,13},{5,1},{9,5},{13,9},{2,14},{6,2},{... | collective-permute-start | bytes 196616 | tf_op jit(solution)/shard_map/ppermute | solution.py:274
  8.8 1.0 %copy-start = (bf16[128,2048]{1,0:T(8,128)(2,1)S(1)}, bf16[128,2048]{1,0:T(8,128)(2,1)}, u32[]{:S(2)}) copy-start(bf16[128,2048]{1,0:T(8,128)(2,1)} %queries.3) | copy-start | bytes 1572868
  9.9 1.0 %copy-start.2 = (bf16[128,2048]{1,0:T(8,128)(2,1)S(1)}, bf16[128,2048]{1,0:T(8,128)(2,1)}, u32[]{:S(2)}) copy-start(bf16[128,2048]{1,0:T(8,128)(2,1)} %out_grad.3) | copy-start | bytes 1572868
  11.0 10.9 %collective-permute-start = (bf16[128,1024]{1,0:T(8,128)(2,1)S(1)}, bf16[128,1024]{1,0:T(8,128)(2,1)S(1)}, u32[]{:S(2)}, u32[]{:S(2)}) collective-permute-start(bf16[128,1024]{1,0:T(8,128)(2,1)S(1)} %get-tuple-element.16), channel_id=1, source_target_pairs={{0,8},{4,12},{8,0},{12,4},{1,9},{5,13},{9,1},{13,5},{2,10},{6,14},... | collective-permute-start | bytes 786440 | tf_op jit(solution)/shard_map/ppermute | solution.py:274
  11.2 7.3 %collective-permute-start.6 = (bf16[4,128,256]{2,1,0:T(8,128)(2,1)S(1)}, bf16[4,128,256]{2,1,0:T(8,128)(2,1)S(1)}, u32[]{:S(2)}, u32[]{:S(2)}) collective-permute-start(bf16[4,128,256]{2,1,0:T(8,128)(2,1)S(1)} %pad_maximum_fusion.kv00), channel_id=1, source_target_pairs={{0,2},{2,0},{1,3},{3,1},{4,6},{6,4},{5,7},{7,5},{8,10},{10,8},{9,1... | collective-permute-start | bytes 786440 | tf_op jit(solution)/shard_map/ppermute | solution.py:278
  12.8 12.6 %collective-permute-start.1 = (bf16[128,1024]{1,0:T(8,128)(2,1)S(1)}, bf16[128,1024]{1,0:T(8,128)(2,1)S(1)}, u32[]{:S(2)}, u32[]{:S(2)}) collective-permute-start(bf16[128,1024]{1,0:T(8,128)(2,1)S(1)} %get-tuple-element.17), channel_id=1, source_target_pairs={{0,4},{4,8},{8,12},{12,0},{1,5},{5,9},{9,13},{13,1},{2,6},{6,10},{... | collective-permute-start | bytes 786440 | tf_op jit(solution)/shard_map/ppermute | solution.py:274
  13.7 11.8 %copy-start.1 = (bf16[128,2048]{1,0:T(8,128)(2,1)S(1)}, bf16[128,2048]{1,0:T(8,128)(2,1)}, u32[]{:S(2)}) copy-start(bf16[128,2048]{1,0:T(8,128)(2,1)} %queries.3) | copy-start | bytes 1572868
  13.7 11.8 %copy-start.3 = (bf16[128,2048]{1,0:T(8,128)(2,1)S(1)}, bf16[128,2048]{1,0:T(8,128)(2,1)}, u32[]{:S(2)}) copy-start(bf16[128,2048]{1,0:T(8,128)(2,1)} %out_grad.3) | copy-start | bytes 1572868
  13.7 11.8 %copy-start.6 = (s32[32]{0:T(128)S(1)}, s32[32]{0:T(128)}, u32[]{:S(2)}) copy-start(s32[32]{0:T(128)} %spans.1) | copy-start | bytes 388
  13.7 11.7 %collective-permute-start.2 = (bf16[128,1024]{1,0:T(8,128)(2,1)S(1)}, bf16[128,1024]{1,0:T(8,128)(2,1)S(1)}, u32[]{:S(2)}, u32[]{:S(2)}) collective-permute-start(bf16[128,1024]{1,0:T(8,128)(2,1)S(1)} %get-tuple-element.18), channel_id=1, source_target_pairs={{0,12},{4,0},{8,4},{12,8},{1,13},{5,1},{9,5},{13,9},{2,14},{6,2},{... | collective-permute-start | bytes 786440 | tf_op jit(solution)/shard_map/ppermute | solution.py:274
  16.1 9.3 %collective-permute-start.7 = (bf16[4,128,256]{2,1,0:T(8,128)(2,1)S(1)}, bf16[4,128,256]{2,1,0:T(8,128)(2,1)S(1)}, u32[]{:S(2)}, u32[]{:S(2)}) collective-permute-start(bf16[4,128,256]{2,1,0:T(8,128)(2,1)S(1)} %pad_maximum_fusion.kv00), channel_id=1, source_target_pairs={{0,1},{1,0},{2,3},{3,2},{4,5},{5,4},{6,7},{7,6},{8,9},{9,8},{10,11... | collective-permute-start | bytes 786440 | tf_op jit(solution)/shard_map/ppermute | solution.py:278
  18.5 7.0 %collective-permute-start.8 = (bf16[4,128,256]{2,1,0:T(8,128)(2,1)S(1)}, bf16[4,128,256]{2,1,0:T(8,128)(2,1)S(1)}, u32[]{:S(2)}, u32[]{:S(2)}) collective-permute-start(bf16[4,128,256]{2,1,0:T(8,128)(2,1)S(1)} %collective-permute-done.6.kv10), channel_id=1, source_target_pairs={{0,1},{1,0},{2,3},{3,2},{4,5},{5,4},{6,7},{7,6},{8,9},{9,8},{10,11... | collective-permute-start | bytes 786440 | tf_op jit(solution)/shard_map/ppermute | solution.py:278
  36.0 2.5 %collective-permute-start.12 = (bf16[8,128,256]{2,1,0:T(8,128)(2,1)S(1)}, bf16[8,128,256]{2,1,0:T(8,128)(2,1)S(1)}, u32[]{:S(2)}, u32[]{:S(2)}) collective-permute-start(bf16[8,128,256]{2,1,0:T(8,128)(2,1)S(1)} %get-tuple-element.28), channel_id=1, source_target_pairs={{0,1},{1,0},{2,3},{3,2},{4,5},{5,4},{6,7},{7,6},{8,9},{9,8},{10,11... | collective-permute-start | bytes 1572872 | tf_op jit(solution)/shard_map/ppermute | solution.py:278
  36.1 11.8 %collective-permute-start.9 = (bf16[128,512]{1,0:T(8,128)(2,1)S(1)}, bf16[128,512]{1,0:T(8,128)(2,1)S(1)}, u32[]{:S(2)}, u32[]{:S(2)}) collective-permute-start(bf16[128,512]{1,0:T(8,128)(2,1)S(1)} %get-tuple-element.24), channel_id=1, source_target_pairs={{0,8},{4,12},{8,0},{12,4},{1,9},{5,13},{9,1},{13,5},{2,10},{6,14},... | collective-permute-start | bytes 393224 | tf_op jit(solution)/shard_map/ppermute | solution.py:274
  36.4 11.5 %collective-permute-start.10 = (bf16[128,512]{1,0:T(8,128)(2,1)S(1)}, bf16[128,512]{1,0:T(8,128)(2,1)S(1)}, u32[]{:S(2)}, u32[]{:S(2)}) collective-permute-start(bf16[128,512]{1,0:T(8,128)(2,1)S(1)} %get-tuple-element.25), channel_id=1, source_target_pairs={{0,12},{4,0},{8,4},{12,8},{1,13},{5,1},{9,5},{13,9},{2,14},{6,2},{... | collective-permute-start | bytes 393224 | tf_op jit(solution)/shard_map/ppermute | solution.py:274
  38.2 9.7 %collective-permute-start.11 = (bf16[128,512]{1,0:T(8,128)(2,1)S(1)}, bf16[128,512]{1,0:T(8,128)(2,1)S(1)}, u32[]{:S(2)}, u32[]{:S(2)}) collective-permute-start(bf16[128,512]{1,0:T(8,128)(2,1)S(1)} %get-tuple-element.26), channel_id=1, source_target_pairs={{0,4},{4,8},{8,12},{12,0},{1,5},{5,9},{9,13},{13,1},{2,6},{6,10},{... | collective-permute-start | bytes 393224 | tf_op jit(solution)/shard_map/ppermute | solution.py:274
  39.4 17.4 %all-to-all-start = ((bf16[8,128,256]{2,1,0:T(8,128)(2,1)}), bf16[8,128,256]{2,1,0:T(8,128)(2,1)S(1)}, u32[]{:S(2)}, u32[]{:S(2)}) async-start(bf16[8,128,256]{2,1,0:T(8,128)(2,1)} %add_convert_fusion), calls=%async_computation | async-start | bytes 1048576 | tf_op jit(solution)/shard_map/all_to_all | solution.py:297
